TPU v7x, 32 devices: a whole 2x2x4 slice. The times are simulated.
32 devices in a mesh: row: 4 (over y, core), col: 8 (over z, x).
Axes of the slice: x: 2, y: 2, z: 4, core: 2. Of those that a mesh axis runs over, the one named last changes fastest.
Arguments:
- ancestor_inverse: float32 [12288, 12288], P('row', 'col')
- factor: bfloat16 [3, 12288, 512], P(None, ('row', 'col')), may hold values from -0.5 to 0.5
- coupling: float32 [3, 512, 512], replicated, may hold values from -0.25 to 0.25
- diagonal_inverse: float32 [3, 512, 512], replicated, may hold values from -6 to 6
- ancestors: int32 [3, 24], replicated, may hold values from -1 to 23, as said below
Outputs:
- block_columns: float32 [3, 12288, 512], P(None, ('row', 'col'))
- block_rows: float32 [3, 12288, 512], P(None, ('col', 'row'))
- node_blocks: float32 [3, 3, 512, 512], replicated
Inputs may be any that keep to these rules, and one draw needn't show every extreme that they name: `ancestors`: row k lists the ancestor block rows of supernode k, blocks of 512 rows: distinct indices in increasing order, then -1 in the slots left. Every block is listed by some supernode.
All inputs are finite; a program needn't handle non-finite values.
Results may differ from a plain program's by a relative error of at most 0.0003.
Values may be sent and summed in bfloat16 or wider, within the bound.
No kernel may reach another device: no remote copies, remote signals or barrier semaphores. Data moves between devices by JAX's collectives and lax.ppermute only.
A program may use at most 128 MiB of HBM per device.

v0:
```python
import functools

import jax
import jax.numpy as jnp
from jax import lax
from jax.experimental import pallas as pl
from jax.experimental.pallas import tpu as pltpu
from jax.sharding import PartitionSpec as P

both = ("row", "col")
high = lax.Precision.HIGH


def matmul(left, right):
    return jnp.dot(left, right, precision=high)


def left_dot(left, right):
    return lax.dot_general(left, right, (((0,), (0,)), ((), ())), precision=high)


def pair_index(later, earlier):
    return later * (later - 1) // 2 + earlier


def split_terms(value):
    head = lax.reduce_precision(value, 8, 7)
    return head.astype(jnp.bfloat16), (value - head).astype(jnp.bfloat16)


def after(value, *others):
    return lax.optimization_barrier((value, *others))[0]


def ring_order(count):
    return list(range(0, count, 2)) + list(range(count - 1, 0, -2))


def ring_moves(order):
    count = len(order)
    ahead = [(order[at], order[(at + 1) % count]) for at in range(count)]
    return ahead, [(target, source) for source, target in ahead]


def ring_step(pieces, moves, last):
    up, down = (pieces[0], pieces[0]) if len(pieces) == 1 else pieces[-2:]
    if last:
        half = up.shape[0] // 2
        up, down = up[:half], down[half:]
    return [*pieces, lax.ppermute(up, "col", moves[0]), lax.ppermute(down, "col", moves[1])]


def ring_sources(order, col_index):
    count = len(order)
    place = [0] * count
    for at, device in enumerate(order):
        place[device] = at
    my_place = jnp.asarray(place, jnp.int32)[col_index]
    table = jnp.asarray(order, jnp.int32)
    steps = [0]
    for step in range(1, count // 2):
        steps += [-step, step]
    steps.append(count // 2)
    return table[(my_place + jnp.asarray(steps, jnp.int32)) % count]


def two_terms(block):
    value = block[...]
    head = value.astype(jnp.bfloat16)
    tail = (value - head.astype(jnp.float32)).astype(jnp.bfloat16)
    return jnp.concatenate([head, tail], axis=0)


def put_double(doubled, piece, span=slice(None)):
    depth = piece.shape[1]
    doubled[span, :depth] = piece[...]
    doubled[span, depth:] = piece[...]


def add_product(doubled, terms, total, first, start):
    cols = total.shape[1]
    count = 3 if cols % 384 == 0 else 1
    span = cols // count

    def add(at, carry):
        here = pl.ds(pl.multiple_of(at * span, span), span)
        part = jnp.dot(doubled[...], terms[:, here], preferred_element_type=jnp.float32)
        begin = jnp.zeros_like(part) if start is None else start[:, here]
        total[:, here] = jnp.where(first, begin, total[:, here]) + part
        return carry

    lax.fori_loop(0, count, add, 0)


def partial_body(nodes, count, resume, sources, *refs):
    pieces = refs[: nodes * count]
    block = refs[nodes * count]
    total, doubled, terms = refs[-3:]
    node, step = pl.program_id(0), pl.program_id(1)
    for at, piece in enumerate(pieces):

        @pl.when((node == at // count) & (step == at % count))
        def _(piece=piece):
            put_double(doubled, piece)

    terms[...] = two_terms(block)
    start = refs[nodes * count + 1] if resume else None
    add_product(doubled, terms, total, step == 0, start)


def final_body(count, lanes, out_piece, sources, core, *refs):
    pieces = refs[: count + 1]
    block, start, given, kept, total, doubled, terms = refs[count + 1 :]
    step = pl.program_id(0)
    for at in range(count - 1):

        @pl.when(step == at)
        def _(at=at):
            put_double(doubled, pieces[at])

    @pl.when(step == count - 1)
    def _():
        half = pieces[count].shape[0]
        put_double(doubled, pieces[count - 1], slice(0, half))
        put_double(doubled, pieces[count], slice(half, 2 * half))

    terms[...] = two_terms(block)
    add_product(doubled, terms, total, step == 0, start)

    @pl.when(step == count - 1)
    def _():
        for lane in range(lanes):
            for side in range(2):
                first = (2 * lane + side) * out_piece

                @pl.when(core[0] == side)
                def _(lane=lane, first=first):
                    kept[lane] = total[:, first : first + out_piece]

                @pl.when(core[0] != side)
                def _(lane=lane, first=first):
                    given[lane] = total[:, first : first + out_piece]


def product_call(body, grid, prefetch, args, in_specs, out_shape, out_specs, scratch, flops, **more):
    return pl.pallas_call(
        body,
        grid_spec=pltpu.PrefetchScalarGridSpec(
            num_scalar_prefetch=prefetch,
            grid=grid,
            in_specs=in_specs,
            out_specs=out_specs,
            scratch_shapes=scratch,
        ),
        out_shape=out_shape,
        compiler_params=pltpu.CompilerParams(
            dimension_semantics=("arbitrary",) * len(grid), vmem_limit_bytes=56 << 20
        ),
        cost_estimate=pl.CostEstimate(
            flops=flops, bytes_accessed=flops // 512, transcendentals=0
        ),
        **more,
    )(*args)


def partial_product(groups, block, sources, start=None):
    nodes, count = len(groups), len(groups[0])
    width, piece = groups[0][0].shape
    cols = block.shape[1]
    pieces = [array for group in groups for array in group]
    total = pl.BlockSpec((None, width, cols), lambda node, step, sources: (node, 0, 0))
    in_specs = [pl.BlockSpec(pieces[0].shape, lambda node, step, sources: (0, 0))] * len(pieces)
    in_specs.append(pl.BlockSpec((piece, cols), lambda node, step, sources: (sources[step], 0)))
    args = [sources, *pieces, block]
    aliases = {}
    if start is not None:
        aliases = {len(args): 0}
        in_specs.append(total)
        args.append(start)
    return product_call(
        functools.partial(partial_body, nodes, count, start is not None),
        (nodes, count), 1, args, in_specs,
        jax.ShapeDtypeStruct((nodes, width, cols), jnp.float32), total,
        [
            pltpu.VMEM((width, 2 * piece), jnp.bfloat16),
            pltpu.VMEM((2 * piece, cols), jnp.bfloat16),
        ],
        4 * nodes * count * width * piece * cols, input_output_aliases=aliases,
    )


def final_product(node, pieces, block, sources, core, lanes, start):
    count = len(pieces) - 1
    width, piece = pieces[0].shape
    cols = block.shape[1]
    out_piece = cols // (2 * lanes)
    half = jax.ShapeDtypeStruct((lanes, width, out_piece), jnp.float32)
    half_spec = pl.BlockSpec(half.shape, lambda step, *_: (0, 0, 0))
    in_specs = [pl.BlockSpec(array.shape, lambda step, *_: (0, 0)) for array in pieces]
    in_specs.append(pl.BlockSpec((piece, cols), lambda step, sources, core: (sources[step], 0)))
    in_specs.append(pl.BlockSpec((None, width, cols), lambda step, *_: (node, 0, 0)))
    return product_call(
        functools.partial(final_body, count, lanes, out_piece), (count,), 2,
        [sources, core, *pieces, block, start], in_specs, [half, half], [half_spec, half_spec],
        [
            pltpu.VMEM((width, cols), jnp.float32),
            pltpu.VMEM((width, 2 * piece), jnp.bfloat16),
            pltpu.VMEM((2 * piece, cols), jnp.bfloat16),
        ],
        4 * count * width * piece * cols,
    )


pad_rows = 16


def step_of(lanes):
    return 128 if lanes % 128 == 0 else lanes


def encoded(value):
    top = jnp.max(jnp.abs(value), axis=-2, keepdims=True)
    exponent = jnp.ceil(jnp.log2(jnp.maximum(top, 1e-30)) + 0.01)
    whole = jnp.round(value * jnp.exp2(15.0 - exponent)).astype(jnp.int32)
    wide = jnp.broadcast_to(exponent, (pad_rows, value.shape[-1])).astype(jnp.int32)
    return whole.astype(jnp.int16), wide.astype(jnp.int16)


def put_coded(ref, value, lead=()):
    rows = value.shape[0]
    whole, wide = encoded(value)
    ref[(*lead, slice(0, rows), slice(None))] = whole
    ref[(*lead, slice(rows, rows + pad_rows), slice(None))] = wide


def get_coded(ref, lead=()):
    rows = ref.shape[-2] - pad_rows
    whole = ref[(*lead, slice(0, rows), slice(None))].astype(jnp.int32).astype(jnp.float32)
    wide = ref[(*lead, slice(rows, rows + pad_rows), slice(None))].astype(jnp.int32)
    return whole * jnp.exp2(wide.astype(jnp.float32)[0:1, :] - 15.0)


def simple_call(body, args, in_specs, out_shape, out_specs, grid, prefetch=0, **more):
    size = sum(array.size * array.dtype.itemsize for array in args)
    return pl.pallas_call(
        body,
        grid_spec=pltpu.PrefetchScalarGridSpec(
            num_scalar_prefetch=prefetch,
            grid=grid,
            in_specs=in_specs,
            out_specs=out_specs,
            scratch_shapes=more.pop("scratch_shapes", ()),
        ),
        out_shape=out_shape,
        compiler_params=pltpu.CompilerParams(
            dimension_semantics=("arbitrary",) * len(grid), vmem_limit_bytes=48 << 20
        ),
        cost_estimate=pl.CostEstimate(flops=size, bytes_accessed=size, transcendentals=0),
        **more,
    )(*args)


def prepare_body(nodes, block_rows, first_row, ancestors, *refs):
    source, outs = refs[0], refs[1:]
    rows = source.shape[1]
    slots = ancestors.shape[1]
    row = lax.broadcasted_iota(jnp.int32, (rows, 1), 0) + first_row[0]
    first_block = lax.div(first_row[0], block_rows)
    for node in range(nodes):
        keep = None
        for ahead in range((rows - 1) // block_rows + 2):
            block = first_block + ahead
            listed = ancestors[node, 0] == block
            for slot in range(1, slots):
                listed = listed | (ancestors[node, slot] == block)
            inside = (row >= block * block_rows) & (row < (block + 1) * block_rows) & listed
            keep = inside if keep is None else keep | inside
        value = jnp.where(keep, source[node].astype(jnp.float32), 0.0)
        turned = value.T.astype(jnp.bfloat16)
        outs[node][...] = turned
        outs[nodes][node] = turned


def prepare(factor, ancestors, first_row):
    nodes, rows, width = factor.shape
    shape = jax.ShapeDtypeStruct((width, rows), jnp.bfloat16)
    spec = pl.BlockSpec((width, rows), lambda at, *_: (0, 0))
    return simple_call(
        functools.partial(prepare_body, nodes, width),
        [first_row, ancestors, factor],
        [pl.BlockSpec(factor.shape, lambda at, *_: (0, 0, 0))],
        [shape] * nodes + [jax.ShapeDtypeStruct((nodes, width, rows), jnp.bfloat16)],
        [spec] * nodes + [pl.BlockSpec((nodes, width, rows), lambda at, *_: (0, 0, 0))],
        (1,), 2,
    )


def add_encode_body(shifts, lane, *refs):
    total = refs[2 * (shifts + 1)]
    total[...] = refs[0][...] + refs[1][...]
    for at in range(shifts):
        value = refs[2 * at + 2][...] + refs[2 * at + 3][...]
        put_coded(refs[2 * (shifts + 1) + 1 + at], value)


def add_encode(kept, other, lane, lanes):
    _, rows, width = kept.shape
    lane_step = step_of(width)
    in_specs, args = [], []
    for shift in range(lanes):
        spec = pl.BlockSpec(
            (None, rows, lane_step),
            lambda at, lane, shift=shift: (lax.rem(lane[0] + shift, lanes), 0, at),
        )
        in_specs += [spec, spec]
        args += [kept, other]
    out_specs = [pl.BlockSpec((rows, lane_step), lambda at, lane: (0, at))]
    out_shape = [jax.ShapeDtypeStruct((rows, width), jnp.float32)]
    for _ in range(1, lanes):
        out_specs.append(pl.BlockSpec((rows + pad_rows, lane_step), lambda at, lane: (0, at)))
        out_shape.append(jax.ShapeDtypeStruct((rows + pad_rows, width), jnp.int16))
    return simple_call(
        functools.partial(add_encode_body, lanes - 1), [lane, *args], in_specs,
        out_shape, out_specs, (width // lane_step,), 1,
    )


def split_dots(pairs):
    total = None
    for (left_head, left_tail), right in pairs:
        right_head = right.astype(jnp.bfloat16)
        right_tail = (right - right_head.astype(jnp.float32)).astype(jnp.bfloat16)
        for left, value in ((left_tail, right_head), (left_head, right_tail), (left_head, right_head)):
            part = jnp.dot(left, value, preferred_element_type=jnp.float32)
            total = part if total is None else total + part
    return total


def chain_body(node, lanes, *refs):
    mine, *received = refs[:lanes]
    heads = refs[lanes : lanes + node]
    tails = refs[lanes + node : lanes + 2 * node]
    earlier = refs[lanes + 2 * node : lanes + 3 * node]
    value, coded, turned = refs[-3:]
    total = mine[...]
    for ref in received:
        total = total + get_coded(ref)
    if node:
        total = total + split_dots(
            [((h[...], t[...]), e[...]) for h, t, e in zip(heads, tails, earlier, strict=True)]
        )
    total = -total
    value[...] = total
    put_coded(coded, total)
    turned[...] = total.T


def chain(node, nodes, mine, received, heads, tails, earlier, turned):
    rows, width = mine.shape
    lane_step = step_of(width)
    lanes = 1 + len(received)
    first = node * (node - 1) // 2
    column = lambda rows: pl.BlockSpec((rows, lane_step), lambda at: (0, at))
    in_specs = [column(rows)] + [column(rows + pad_rows)] * len(received)
    factor_specs = [
        pl.BlockSpec((None, rows, rows), lambda at, j=j: (first + j, 0, 0)) for j in range(node)
    ]
    in_specs += factor_specs + factor_specs + [column(rows)] * node
    args = [mine, *received, *[heads] * node, *[tails] * node, *earlier]
    aliases = {}
    if turned is not None:
        aliases = {len(args): 2}
        args.append(turned)
        in_specs.append(pl.BlockSpec(memory_space=pl.ANY))
    return simple_call(
        functools.partial(chain_body, node, lanes), args, in_specs,
        [
            jax.ShapeDtypeStruct((rows, width), jnp.float32),
            jax.ShapeDtypeStruct((rows + pad_rows, width), jnp.int16),
            jax.ShapeDtypeStruct((nodes, width, rows), jnp.float32),
        ],
        [
            column(rows),
            column(rows + pad_rows),
            pl.BlockSpec((None, lane_step, rows), lambda at: (node, at, 0)),
        ],
        (width // lane_step,), input_output_aliases=aliases,
    )


def turn_body(*refs):
    refs[-1][...] = get_coded(refs[0]).T


def turn(node, nodes, coded, turned):
    padded, width = coded.shape
    lane_step = step_of(width)
    rows = padded - pad_rows
    args, in_specs = [coded], [pl.BlockSpec((padded, lane_step), lambda at: (0, at))]
    aliases = {}
    if turned is not None:
        aliases = {1: 0}
        args.append(turned)
        in_specs.append(pl.BlockSpec(memory_space=pl.ANY))
    return simple_call(
        turn_body, args, in_specs,
        jax.ShapeDtypeStruct((nodes, width, rows), jnp.float32),
        pl.BlockSpec((None, lane_step, rows), lambda at: (node, at, 0)),
        (width // lane_step,), input_output_aliases=aliases,
    )


def inner_body(half, low, up, left, rows, mine, given):
    value = rows[...]
    head = value.astype(jnp.bfloat16)
    tail = (value - head.astype(jnp.float32)).astype(jnp.bfloat16)
    value = jnp.dot(
        left[...], jnp.concatenate([head, tail, head], axis=0), preferred_element_type=jnp.float32
    )

    @pl.when(pl.program_id(0) < half)
    def _():
        mine[...] = value

    @pl.when(pl.program_id(0) >= half)
    def _():
        given[...] = value


def inner(low, up, left, rows):
    nodes, piece, width = rows.shape
    count = nodes * (nodes + 1) // 2
    half = count // 2
    shape = jax.ShapeDtypeStruct((half, width, width), jnp.float32)
    return simple_call(
        functools.partial(inner_body, half), [low, up, left, rows],
        [
            pl.BlockSpec((None, width, left.shape[2]), lambda at, low, up: (low[at], 0, 0)),
            pl.BlockSpec((None, piece, width), lambda at, low, up: (up[at], 0, 0)),
        ],
        [shape, shape],
        [
            pl.BlockSpec((None, width, width), lambda at, *_: (jnp.minimum(at, half - 1), 0, 0)),
            pl.BlockSpec((None, width, width), lambda at, *_: (jnp.maximum(at - half, 0), 0, 0)),
        ],
        (count,), 2,
    )


def deal_body(plain, coded, count, starts, *refs):
    total = refs[0][...]
    for ref in refs[1:plain]:
        total = total + ref[...]
    for ref in refs[plain : plain + coded]:
        total = total + get_coded(ref)
    outs = refs[plain + coded :]
    if count == 1:
        put_coded(outs[0], total)
        return
    whole = outs[-1]
    whole[...] = total
    rows = total.shape[0] // count
    for at in range(count):
        part = whole[pl.ds(pl.multiple_of(starts[at], 8), rows), :]
        if at == 0:
            outs[0][...] = part
        else:
            put_coded(outs[at], part)


def deal(plain, coded, starts):
    rows, width = plain[0].shape
    lane_step = step_of(width)
    count = starts.shape[0]
    column = lambda rows: pl.BlockSpec((rows, lane_step), lambda at, starts: (0, at))
    part = rows // count
    shapes = [jax.ShapeDtypeStruct((part, width), jnp.float32)] if count > 1 else []
    shapes += [jax.ShapeDtypeStruct((part + pad_rows, width), jnp.int16)] * max(count - 1, 1)
    return simple_call(
        functools.partial(deal_body, len(plain), len(coded), count),
        [starts, *plain, *coded],
        [column(rows)] * len(plain) + [column(rows + pad_rows)] * len(coded),
        shapes, [column(shape.shape[0]) for shape in shapes], (width // lane_step,), 1,
        scratch_shapes=[pltpu.VMEM((rows, lane_step), jnp.float32)] if count > 1 else [],
    )


def heap_body(*refs):
    for at, ref in enumerate(refs[:-1]):
        refs[-1][at] = ref[...]


def heap(parts):
    rows, width = parts[0].shape
    lane_step = step_of(width)
    return simple_call(
        heap_body, parts,
        [pl.BlockSpec((rows, lane_step), lambda at: (0, at))] * len(parts),
        jax.ShapeDtypeStruct((len(parts), rows, width), parts[0].dtype),
        pl.BlockSpec((len(parts), rows, lane_step), lambda at: (0, 0, at)),
        (width // lane_step,),
    )


def finish_body(arrays, width, place, row_of, col_of, *refs):
    parts = refs[:arrays]
    base, out, sums = refs[arrays:]
    step = pl.program_id(0)
    count, padded, _ = parts[0].shape
    rows = padded - pad_rows

    @pl.when(step == 0)
    def _():
        for at, ref in enumerate(parts):

            def put(piece, carry, at=at, ref=ref):
                start = pl.multiple_of(place[at * count + piece], 8)
                sums[pl.ds(start, rows), :] = get_coded(ref, (piece,))
                return carry

            lax.fori_loop(0, count, put, 0)

    row, col = row_of[step], col_of[step]
    low, up = jnp.minimum(row, col), jnp.maximum(row, col)
    start = pl.multiple_of((up * (up + 1) // 2 + low) * width, width)
    value = base[...] - sums[pl.ds(start, width), :]

    @pl.when(row <= col)
    def _():
        out[...] = value

    @pl.when(row > col)
    def _():
        out[...] = value.T


def finish(place, parts, base, nodes, width):
    visits = []
    for up in range(nodes):
        for low in range(up):
            visits += [(low, up), (up, low)]
        visits.append((up, up))
    row_of = jnp.asarray([row for row, _ in visits], jnp.int32)
    col_of = jnp.asarray([col for _, col in visits], jnp.int32)

    def base_map(step, place, row_of, col_of):
        low = jnp.minimum(row_of[step], col_of[step])
        up = jnp.maximum(row_of[step], col_of[step])
        return (up * (up + 1) // 2 + low, 0, 0)

    whole = pl.BlockSpec(parts[0].shape, lambda step, *_: (0, 0, 0))
    return simple_call(
        functools.partial(finish_body, len(parts), width),
        [place, row_of, col_of, *parts, base],
        [whole] * len(parts) + [pl.BlockSpec((None, width, width), base_map)],
        jax.ShapeDtypeStruct((nodes, nodes, width, width), jnp.float32),
        pl.BlockSpec(
            (None, None, width, width),
            lambda step, place, row_of, col_of: (row_of[step], col_of[step], 0, 0),
        ),
        (nodes * nodes,), 3,
        scratch_shapes=[pltpu.VMEM((nodes * (nodes + 1) // 2 * width, width), jnp.float32)],
    )


def spread_bits(number, bits):
    return sum(((number >> at) & 1) << bit for at, bit in enumerate(bits))


def gather_bits(index, bits):
    return sum(((index >> bit) & 1) << at for at, bit in enumerate(bits))


def local(ancestor_inverse, factor, coupling, diagonal_inverse, ancestors):
    row_count = lax.axis_size("row")
    col_count = lax.axis_size("col")
    total = row_count * col_count
    row_index = lax.axis_index("row")
    col_index = lax.axis_index("col")
    flat_index = row_index * col_count + col_index
    nodes, piece_rows, width = factor.shape
    col_bits = col_count.bit_length() - 1
    first_row = (flat_index * piece_rows).reshape(1).astype(jnp.int32)
    *lower, lower_stack = prepare(factor, ancestors, first_row)

    order = ring_order(col_count)
    sources = ring_sources(order, col_index)
    core = (row_index % 2).reshape(1).astype(jnp.int32)
    moves = ring_moves(order)
    lanes = row_count // 2
    steps = col_count // 2
    near, early = 3, 1 + 2 * (steps - 2)
    gathered = [[lower[node]] for node in range(nodes)]

    def advance(step):
        for node in range(nodes):
            gathered[node] = ring_step(gathered[node], moves, step == steps)

    for step in range(1, steps - 1):
        advance(step)

    early_coupling = after(coupling, gathered[0][1])
    turned_heads, turned_tails = split_terms(jnp.swapaxes(early_coupling, 1, 2))
    first_pieces = [group[:near] for group in gathered]
    first_pieces[0][0], turned_heads, turned_tails = lax.optimization_barrier(
        (first_pieces[0][0], turned_heads, turned_tails)
    )
    starts = partial_product(first_pieces, ancestor_inverse, sources[:near])
    advance(steps - 1)
    starts = partial_product(
        [group[near:early] for group in gathered],
        ancestor_inverse,
        sources[near:early],
        starts,
    )
    advance(steps)

    swap = (1 << col_bits) | 1

    def middle(at):
        low, up = at & 1, (at >> col_bits) & 1
        return at if low == up else at ^ swap

    first_moves = [(at, middle(at)) for at in range(total)]
    last_moves = [
        (middle(r * col_count + c), c * row_count + r)
        for r in range(row_count)
        for c in range(col_count)
    ]
    lower_stack = lax.ppermute(
        lower_stack,
        both,
        [
            (c * row_count + r, r * col_count + c)
            for r in range(row_count)
            for c in range(col_count)
            if c * row_count + r != r * col_count + c
        ],
    )

    lane = row_index // 2
    lane_ref = lane.reshape(1).astype(jnp.int32)
    sibling = [(at, at ^ 1) for at in range(row_count)]
    lane_moves = [
        [(at, (at + 2 * shift) % row_count) for at in range(row_count)]
        for shift in range(1, lanes)
    ]

    def lane_sums(given, kept):
        other = lax.ppermute(given, "row", sibling)
        mine, *coded = add_encode(kept, other, lane_ref, lanes)
        return mine, [
            lax.ppermute(part, "row", moves)
            for part, moves in zip(coded, lane_moves, strict=True)
        ]

    base = {}

    def base_columns(columns, others):
        here, diagonal = lax.optimization_barrier((coupling, diagonal_inverse, *others))[:2]
        for k in columns:
            for j in range(k):
                value = -matmul(base[j, 0], here[pair_index(k, 0)])
                for i in range(1, k):
                    value = value - matmul(base[j, i], here[pair_index(k, i)])
                base[j, k] = value
                base[k, j] = value.T
            value = diagonal[k]
            for j in range(k):
                value = value - left_dot(here[pair_index(k, j)], base[j, k])
            base[k, k] = value

    by_cols = []
    out_cols = out_rows = None
    for k in range(nodes):
        given, kept = final_product(
            k, gathered[k][early:], ancestor_inverse, sources[early:], core, lanes, starts
        )
        row_sums = lane_sums(given, kept)
        if k == nodes - 1:
            base_columns(range(k), by_cols[-1:])
            held = lax.optimization_barrier((row_sums[0], base[k - 1, k - 1]))
            row_sums, base[k - 1, k - 1] = (held[0], row_sums[1]), held[1]
        value, coded, out_cols = chain(
            k, nodes, *row_sums, turned_heads, turned_tails, by_cols, out_cols
        )
        by_cols.append(value)
        coded = lax.ppermute(coded, both, first_moves)
        coded = lax.ppermute(coded, both, last_moves)
        out_rows = turn(k, nodes, coded, out_rows)

    stays = col_index * row_count + row_index == flat_index
    lower_stack, late_coupling, _ = lax.optimization_barrier((lower_stack, coupling, by_cols[-2]))
    mixed = []
    for k in range(nodes):
        value = jnp.where(stays, lower[k], lower_stack[k]).astype(jnp.float32)
        for j in range(k):
            value = value - left_dot(late_coupling[pair_index(k, j)], mixed[j])
        mixed.append(value)
    mixed_heads, mixed_tails = split_terms(jnp.stack(mixed))
    left = jnp.concatenate([mixed_tails, mixed_heads, mixed_heads], axis=2)

    count = nodes * (nodes + 1) // 2
    listing = [(j, k) for k in range(nodes) for j in range(k + 1)]
    turned_listing = listing[count // 2 :] + listing[: count // 2]

    def by_core(at):
        one, two = ([pair[at] for pair in pairs] for pairs in (listing, turned_listing))
        return jnp.where(core[0] == 0, jnp.asarray(one, jnp.int32), jnp.asarray(two, jnp.int32))

    low, up = by_core(0), by_core(1)
    kept, given = inner(low, up, left, out_cols)
    half_rows = kept.shape[0] * width
    kept, given = kept.reshape(half_rows, width), given.reshape(half_rows, width)
    flat_bits = (row_count * col_count).bit_length() - 1
    planes = [[0, *range(col_bits + 1, flat_bits)], list(range(1, col_bits))]
    plane_moves = [
        [[(at, at ^ spread_bits(other, bits)) for at in range(total)] for other in range(1, 1 << len(bits))]
        for bits in planes
    ]
    parts_of = [1 << len(bits) for bits in planes]
    mine_of = [gather_bits(flat_index, bits) for bits in planes]

    def starts_of(level, rows):
        around = mine_of[level] ^ jnp.arange(parts_of[level], dtype=jnp.int32)
        return (around * (rows // parts_of[level])).astype(jnp.int32)

    def exchange(arrays, level):
        return [
            lax.ppermute(array, both, moves)
            for array, moves in zip(arrays, plane_moves[level], strict=True)
        ]

    other = lax.ppermute(given, "row", sibling)
    mine, *coded = deal([kept, other], [], starts_of(0, half_rows))
    coded = exchange(coded, 0)
    base_columns(range(nodes - 1, nodes), [mine])
    base = jnp.stack([base[j, k] for k in range(nodes) for j in range(k + 1)])
    mine, base = lax.optimization_barrier((mine, base))
    mine, *coded = deal([mine], coded, starts_of(1, mine.shape[0]))
    coded = exchange(coded, 1)
    (summed,) = deal([mine], coded, jnp.zeros((1,), jnp.int32))
    pile = heap([summed, *exchange([summed] * (parts_of[1] - 1), 1)])
    piles = [pile, *exchange([pile] * (parts_of[0] - 1), 0)]
    *late, out_rows = lax.optimization_barrier((*piles[2:], out_rows))
    piles = [*piles[:2], *late]
    piles += [lax.ppermute(pile, "row", sibling) for pile in piles]
    rows_at = half_rows // (parts_of[0] * parts_of[1])
    around = [mine_of[at] ^ jnp.arange(parts_of[at], dtype=jnp.int32) for at in range(2)]
    within = (around[0][:, None] * parts_of[1] + around[1][None, :]).reshape(-1) * rows_at
    place = jnp.concatenate(
        [core[0] * half_rows + within, (1 - core[0]) * half_rows + within]
    ).astype(jnp.int32)
    pile, base = lax.optimization_barrier((piles[0], base))
    node_blocks = finish(place, [pile, *piles[1:]], base, nodes, width)
    return out_rows, out_cols, node_blocks


def solution(mesh):
    placed = (P("row", "col"), P(None, both, None), P(), P(), P())

    return jax.shard_map(
        local,
        mesh=mesh,
        in_specs=placed,
        out_specs=(P(None, both, None), P(None, ("col", "row"), None), P()),
        check_vma=False,
    )
```

profile of v0, /device:TPU:0, one launch (start us, length us, event | category | flops | bytes accessed | tf_op | source)
XLA Modules:
  0.0 366.2 jit_solution(17684588619619663667)
XLA Ops:
  4.7 3.1 collective-permute-start.1
  21.4 4.7 %collective-permute-done.9.refs_1_ = bf16[512,384]{1,0:T(8,128)(2,1)} collective-permute-done((bf16[512,384]{1,0:T(8,128)(2,1)S(1)}, bf16[512,384]{1,0:T(8,128)(2,1)}, u32[]{:S(2)}, u32[]{:S(2)}) %collective-permute-start.9) | collective-permute-done | bytes 393248 | tf_op jit(solution)/shard_map/ppermute | solution.py:50
  29.9 4.6 %collective-permute-done.13.refs_7_ = bf16[512,384]{1,0:T(8,128)(2,1)S(1)} collective-permute-done((bf16[512,384]{1,0:T(8,128)(2,1)S(1)}, bf16[512,384]{1,0:T(8,128)(2,1)S(1)}, u32[]{:S(2)}, u32[]{:S(2)}) %collective-permute-start.13) | collective-permute-done | bytes 393248 | tf_op jit(solution)/shard_map/ppermute | solution.py:50
  37.8 3.5 copy.26
  41.3 3.7 %fusion = (bf16[3,512,512]{2,1,0:T(8,128)(2,1)}, bf16[3,512,512]{2,1,0:T(8,128)(2,1)S(1)}) fusion(f32[3,512,512]{1,2,0:T(8,128)} %copy.26), kind=kLoop, calls=%fused_computation.6 | loop fusion | flops 3145728 | bytes 6291456 | tf_op jit(solution)/shard_map/convert_element_type | solution.py:28
  47.3 4.2 %collective-permute-done.10.refs_0_ = bf16[512,384]{1,0:T(8,128)(2,1)} collective-permute-done((bf16[512,384]{1,0:T(8,128)(2,1)}, bf16[512,384]{1,0:T(8,128)(2,1)}, u32[]{:S(2)}, u32[]{:S(2)}) %collective-permute-start.10) | collective-permute-done | bytes 393248 | tf_op jit(solution)/shard_map/ppermute | solution.py:50
  53.6 26.1 %shard_map.158.refs_7_ = f32[3,512,1536]{2,1,0:T(8,128)} custom-call(s32[3]{0:T(128)} %get-tuple-element.115.sources, bf16[512,384]{1,0:T(8,128)(2,1)} %copy-done.4, bf16[512,384]{1,0:T(8,128)(2,1)} %collective-permute-done.9.refs_1_, bf16[512,384]{1,0:T(8,128)(2,1)} %collective-permute-done.11.refs_2_, bf16[512,384]{1,0:T(8,128)(2,1)} %copy-done.11, ...), custom_call_target="tpu_custom_call" | custom-call | flops 10871635968 | bytes 21233664 | tf_op jit(solution)/shard_map/pallas_call | solution.py:146
  86.0 20.0 %shard_map.159.refs_5_ = f32[3,512,1536]{2,1,0:T(8,128)} custom-call(s32[2]{0:T(128)} %slice.73.sources, bf16[512,384]{1,0:T(8,128)(2,1)} %collective-permute-done.10.refs_0_, bf16[512,384]{1,0:T(8,128)(2,1)} %collective-permute-done.12.refs_1_, bf16[512,384]{1,0:T(8,128)(2,1)} %copy-done.35, ...), custom_call_target="tpu_custom_call", output_to_operand_aliasing={{}: (8, {})} | custom-call | flops 7247757312 | bytes 14155776 | tf_op jit(solution)/shard_map/pallas_call | solution.py:146
  111.1 12.1 %shard_map.162 = (f32[2,512,384]{2,1,0:T(8,128)}, f32[2,512,384]{2,1,0:T(8,128)}) custom-call(s32[3]{0:T(128)} %get-tuple-element.116.sources, s32[1]{0:T(128)} %bitcast.3.core, bf16[512,384]{1,0:T(8,128)(2,1)} %copy-done.32, bf16[512,384]{1,0:T(8,128)(2,1)} %copy-done.34, bf16[256,384]{1,0:T(8,128)(2,1)} %copy-done.39, bf16[256,384]{1,0:T(8,128)(2,1)} %copy-done.42, ...), custom_call_target="tpu_custom_call" | custom-call | flops 3623878656 | bytes 7077888 | tf_op jit(solution)/shard_map/pallas_call | solution.py:146
  124.7 12.1 %shard_map.160 = (f32[2,512,384]{2,1,0:T(8,128)}, f32[2,512,384]{2,1,0:T(8,128)}) custom-call(s32[3]{0:T(128)} %get-tuple-element.116.sources, s32[1]{0:T(128)} %bitcast.3.core, bf16[512,384]{1,0:T(8,128)(2,1)} %copy-done.29, bf16[512,384]{1,0:T(8,128)(2,1)} %copy-done.33, bf16[256,384]{1,0:T(8,128)(2,1)} %copy-done.41, bf16[256,384]{1,0:T(8,128)(2,1)} %copy-done.44, ...), custom_call_target="tpu_custom_call" | custom-call | flops 3623878656 | bytes 7077888 | tf_op jit(solution)/shard_map/pallas_call | solution.py:146
  138.6 12.1 %shard_map.166 = (f32[2,512,384]{2,1,0:T(8,128)}, f32[2,512,384]{2,1,0:T(8,128)}) custom-call(s32[3]{0:T(128)} %get-tuple-element.116.sources, s32[1]{0:T(128)} %bitcast.3.core, bf16[512,384]{1,0:T(8,128)(2,1)} %copy-done.30, bf16[512,384]{1,0:T(8,128)(2,1)} %copy-done.31, bf16[256,384]{1,0:T(8,128)(2,1)} %copy-done.40, bf16[256,384]{1,0:T(8,128)(2,1)} %copy-done.43, ...), custom_call_target="tpu_custom_call" | custom-call | flops 3623878656 | bytes 7077888 | tf_op jit(solution)/shard_map/pallas_call | solution.py:146
  152.4 3.2 shard_map.163
  156.5 3.5 collective-permute-start.24
  159.9 3.2 shard_map.161
  169.4 21.0 %collective-permute-done.24.refs_1_ = s16[528,384]{1,0:T(8,128)(2,1)S(1)} collective-permute-done((s16[528,384]{1,0:T(8,128)(2,1)}, s16[528,384]{1,0:T(8,128)(2,1)S(1)}, u32[]{:S(2)}, u32[]{:S(2)}) %collective-permute-start.24) | collective-permute-done | bytes 405536 | tf_op jit(solution)/shard_map/ppermute | solution.py:653
  192.3 6.8 %collective-permute-done.18.refs_1_ = s16[528,384]{1,0:T(8,128)(2,1)} collective-permute-done((s16[528,384]{1,0:T(8,128)(2,1)}, s16[528,384]{1,0:T(8,128)(2,1)}, u32[]{:S(2)}, u32[]{:S(2)}) %collective-permute-start.18) | collective-permute-done | bytes 405536 | tf_op jit(solution)/shard_map/ppermute | solution.py:653
  199.1 4.4 %shard_map.165 = (f32[512,384]{1,0:T(8,128)S(1)}, s16[528,384]{1,0:T(8,128)(2,1)S(1)}, f32[3,384,512]{2,1,0:T(8,128)}) custom-call(f32[512,384]{1,0:T(8,128)S(1)} %copy-done.10, s16[528,384]{1,0:T(8,128)(2,1)} %collective-permute-done.18.refs_1_, bf16[3,512,512]{2,1,0:T(8,128)(2,1)S(1)} %get-tuple-element.66.refs_2_.refs_3_, ...), custom_call_target="tpu_custom_call", output_to_operand_aliasing={{2}: (5, {})} | custom-call | flops 7483392 | bytes 7483392 | tf_op jit(solution)/shard_map/pallas_call | solution.py:245
  215.6 5.4 %shard_map.168 = (f32[512,384]{1,0:T(8,128)}, s16[528,384]{1,0:T(8,128)(2,1)S(1)}, f32[3,384,512]{2,1,0:T(8,128)}) custom-call(f32[512,384]{1,0:T(8,128)S(1)} %get-tuple-element.82.refs_0_, s16[528,384]{1,0:T(8,128)(2,1)S(1)} %collective-permute-done.30.refs_1_, ...), custom_call_target="tpu_custom_call", output_to_operand_aliasing={{2}: (8, {})} | custom-call | flops 11415552 | bytes 11415552 | tf_op jit(solution)/shard_map/pallas_call | solution.py:245
  222.8 9.6 %shard_map.169 = (f32[3,512,512]{2,1,0:T(8,128)S(1)}, f32[3,512,512]{2,1,0:T(8,128)}) custom-call(s32[6]{0:T(128)S(1)} %get-tuple-element.124.low, s32[6]{0:T(128)S(1)} %get-tuple-element.123.up, bf16[3,512,1152]{2,1,0:T(8,128)(2,1)} %pad_maximum_fusion.left, f32[3,384,512]{2,1,0:T(8,128)S(1)} %copy-done), custom_call_target="tpu_custom_call" | custom-call | flops 5898288 | bytes 5898288 | tf_op jit(solution)/shard_map/pallas_call | solution.py:245
  232.5 4.9 %collective-permute-start.47 = (s16[528,384]{1,0:T(8,128)(2,1)}, s16[528,384]{1,0:T(8,128)(2,1)}, u32[]{:S(2)}, u32[]{:S(2)}) collective-permute-start(s16[528,384]{1,0:T(8,128)(2,1)} %copy-done.20), channel_id=1, source_target_pairs={{0,0},{1,8},{2,2},{3,10},{4,4},{5,12},{6,6},{7,14},{8,1},{9,9},{10... | collective-permute-start | bytes 1216520 | tf_op jit(solution)/shard_map/ppermute | solution.py:688
  239.6 4.4 %shard_map.170 = (f32[384,512]{1,0:T(8,128)S(1)}, s16[400,512]{1,0:T(8,128)(2,1)S(1)}, s16[400,512]{1,0:T(8,128)(2,1)S(1)}, s16[400,512]{1,0:T(8,128)(2,1)S(1)}) custom-call(s32[4]{0:T(128)S(1)} %fusion.35.starts, f32[1536,512]{1,0:T(8,128)S(1)} %bitcast.93, f32[1536,512]{1,0:T(8,128)} %collective-permute-done.31.refs_1_), custom_call_target="tpu_custom_call" | custom-call | flops 6291472 | bytes 6291472 | tf_op jit(solution)/shard_map/pallas_call | solution.py:245
  246.3 5.2 %collective-permute-start.32 = (s16[400,512]{1,0:T(8,128)(2,1)S(1)}, s16[400,512]{1,0:T(8,128)(2,1)S(1)}, u32[]{:S(2)}, u32[]{:S(2)}) collective-permute-start(s16[400,512]{1,0:T(8,128)(2,1)S(1)} %get-tuple-element.93), channel_id=1, source_target_pairs={{0,1},{1,0},{2,3},{3,2},{4,5},{5,4},{6,7},{7,6},{8,9},{9,8},{10,11... | collective-permute-start | bytes 1228808 | tf_op jit(solution)/shard_map/ppermute | solution.py:730
  260.9 11.4 %collective-permute-done.33.refs_2_ = s16[400,512]{1,0:T(8,128)(2,1)S(1)} collective-permute-done((s16[400,512]{1,0:T(8,128)(2,1)S(1)}, s16[400,512]{1,0:T(8,128)(2,1)S(1)}, u32[]{:S(2)}, u32[]{:S(2)}) %collective-permute-start.33) | collective-permute-done | bytes 409632 | tf_op jit(solution)/shard_map/ppermute | solution.py:730
  277.1 3.1 collective-permute-start.36
  280.2 5.6 %collective-permute-start.37 = (s16[112,512]{1,0:T(8,128)(2,1)S(1)}, s16[112,512]{1,0:T(8,128)(2,1)S(1)}, u32[]{:S(2)}, u32[]{:S(2)}) collective-permute-start(s16[112,512]{1,0:T(8,128)(2,1)S(1)} %get-tuple-element.99), channel_id=1, source_target_pairs={{0,6},{1,7},{2,4},{3,5},{4,2},{5,3},{6,0},{7,1},{8,14},{9,15},{10,... | collective-permute-start | bytes 344072 | tf_op jit(solution)/shard_map/ppermute | solution.py:730
  285.8 6.8 %collective-permute-done.36.refs_2_ = s16[112,512]{1,0:T(8,128)(2,1)S(1)} collective-permute-done((s16[112,512]{1,0:T(8,128)(2,1)S(1)}, s16[112,512]{1,0:T(8,128)(2,1)S(1)}, u32[]{:S(2)}, u32[]{:S(2)}) %collective-permute-start.36) | collective-permute-done | bytes 114720 | tf_op jit(solution)/shard_map/ppermute | solution.py:730
  292.6 7.2 %collective-permute-done.37.refs_3_ = s16[112,512]{1,0:T(8,128)(2,1)S(1)} collective-permute-done((s16[112,512]{1,0:T(8,128)(2,1)S(1)}, s16[112,512]{1,0:T(8,128)(2,1)S(1)}, u32[]{:S(2)}, u32[]{:S(2)}) %collective-permute-start.37) | collective-permute-done | bytes 114720 | tf_op jit(solution)/shard_map/ppermute | solution.py:730
  301.5 3.7 %collective-permute-done.38.refs_1_ = s16[112,512]{1,0:T(8,128)(2,1)S(1)} collective-permute-done((s16[112,512]{1,0:T(8,128)(2,1)S(1)}, s16[112,512]{1,0:T(8,128)(2,1)S(1)}, u32[]{:S(2)}, u32[]{:S(2)}) %collective-permute-start.38) | collective-permute-done | bytes 114720 | tf_op jit(solution)/shard_map/ppermute | solution.py:730
  305.2 8.0 %collective-permute-done.39.refs_2_ = s16[112,512]{1,0:T(8,128)(2,1)S(1)} collective-permute-done((s16[112,512]{1,0:T(8,128)(2,1)S(1)}, s16[112,512]{1,0:T(8,128)(2,1)S(1)}, u32[]{:S(2)}, u32[]{:S(2)}) %collective-permute-start.39) | collective-permute-done | bytes 114720 | tf_op jit(solution)/shard_map/ppermute | solution.py:730
  313.6 4.4 %collective-permute-start.42 = (s16[4,112,512]{2,1,0:T(8,128)(2,1)S(1)}, s16[4,112,512]{2,1,0:T(8,128)(2,1)S(1)}, u32[]{:S(2)}, u32[]{:S(2)}) collective-permute-start(s16[4,112,512]{2,1,0:T(8,128)(2,1)S(1)} %shard_map.173.refs_0_), channel_id=1, source_target_pairs={{0,17},{1,16},{2,19},{3,18},{4,21},{5,20},{6,23},{7,22},{8,25},{9,... | collective-permute-start | bytes 1376264 | tf_op jit(solution)/shard_map/ppermute | solution.py:730
  324.7 25.7 %collective-permute-start.50 = (s16[4,112,512]{2,1,0:T(8,128)(2,1)S(1)}, s16[4,112,512]{2,1,0:T(8,128)(2,1)S(1)}, u32[]{:S(2)}, u32[]{:S(2)}) collective-permute-start(s16[4,112,512]{2,1,0:T(8,128)(2,1)S(1)} %shard_map.173.refs_0_), channel_id=1, source_target_pairs={{0,8},{8,0},{16,24},{24,16},{1,9},{9,1},{17,25},{25,17},{2,10},{10... | collective-permute-start | bytes 1376264 | tf_op jit(solution)/shard_map/ppermute | solution.py:747
  354.6 11.6 %shard_map.177 = f32[3,3,512,512]{3,2,1,0:T(8,128)} custom-call(s32[32]{0:T(128)S(1)} %pad_add_fusion.place, s32[9]{0:T(128)S(1)} %copy-done.16, s32[9]{0:T(128)S(1)} %copy-done.17, s16[4,112,512]{2,1,0:T(8,128)(2,1)S(1)} %shard_map.173.refs_0_, s16[4,112,512]{2,1,0:T(8,128)(2,1)S(1)} %collective-permute-done.49.refs_1_, ...), custom_call_target="tpu_custom_call" | custom-call | flops 9961672 | bytes 9961672 | tf_op jit(solution)/shard_map/pallas_call | solution.py:245
  (231 shorter events, 99.7 us)
Async XLA Ops:
  9.8 24.7 %collective-permute-start.13 = (bf16[512,384]{1,0:T(8,128)(2,1)S(1)}, bf16[512,384]{1,0:T(8,128)(2,1)S(1)}, u32[]{:S(2)}, u32[]{:S(2)}) collective-permute-start(bf16[512,384]{1,0:T(8,128)(2,1)S(1)} %get-tuple-element.59.refs_6_), channel_id=1, source_target_pairs={{0,2},{2,4},{4,6},{6,7},{7,5},{5,3},{3,1},{1,0},{8,10},{10,12},{12... | collective-permute-start | bytes 1179656 | tf_op jit(solution)/shard_map/ppermute | solution.py:50
  17.8 27.3 %collective-permute-start.15 = (bf16[512,384]{1,0:T(8,128)(2,1)S(1)}, bf16[512,384]{1,0:T(8,128)(2,1)}, u32[]{:S(2)}, u32[]{:S(2)}) collective-permute-start(bf16[512,384]{1,0:T(8,128)(2,1)S(1)} %get-tuple-element.59.refs_6_), channel_id=1, source_target_pairs={{2,0},{4,2},{6,4},{7,6},{5,7},{3,5},{1,3},{0,1},{10,8},{12,10},{14... | collective-permute-start | bytes 1179656 | tf_op jit(solution)/shard_map/ppermute | solution.py:50
  19.9 25.3 %collective-permute-start.2 = (bf16[512,384]{1,0:T(8,128)(2,1)}, bf16[512,384]{1,0:T(8,128)(2,1)S(1)}, u32[]{:S(2)}, u32[]{:S(2)}) collective-permute-start(bf16[512,384]{1,0:T(8,128)(2,1)} %collective-permute-done.1.refs_4_), channel_id=1, source_target_pairs={{0,2},{2,4},{4,6},{6,7},{7,5},{5,3},{3,1},{1,0},{8,10},{10,12},{12... | collective-permute-start | bytes 1179656 | tf_op jit(solution)/shard_map/ppermute | solution.py:50
  26.2 20.9 %collective-permute-start.5 = (bf16[512,384]{1,0:T(8,128)(2,1)}, bf16[512,384]{1,0:T(8,128)(2,1)S(1)}, u32[]{:S(2)}, u32[]{:S(2)}) collective-permute-start(bf16[512,384]{1,0:T(8,128)(2,1)} %collective-permute-done.4.refs_5_), channel_id=1, source_target_pairs={{2,0},{4,2},{6,4},{7,6},{5,7},{3,5},{1,3},{0,1},{10,8},{12,10},{14... | collective-permute-start | bytes 1179656 | tf_op jit(solution)/shard_map/ppermute | solution.py:50
  28.3 23.2 %collective-permute-start.10 = (bf16[512,384]{1,0:T(8,128)(2,1)}, bf16[512,384]{1,0:T(8,128)(2,1)}, u32[]{:S(2)}, u32[]{:S(2)}) collective-permute-start(bf16[512,384]{1,0:T(8,128)(2,1)} %collective-permute-done.9.refs_1_), channel_id=1, source_target_pairs={{0,2},{2,4},{4,6},{6,7},{7,5},{5,3},{3,1},{1,0},{8,10},{10,12},{12... | collective-permute-start | bytes 1179656 | tf_op jit(solution)/shard_map/ppermute | solution.py:50
  45.1 34.6 %collective-permute-start.14 = (bf16[512,384]{1,0:T(8,128)(2,1)S(1)}, bf16[512,384]{1,0:T(8,128)(2,1)S(1)}, u32[]{:S(2)}, u32[]{:S(2)}) collective-permute-start(bf16[512,384]{1,0:T(8,128)(2,1)S(1)} %copy-done.47), channel_id=1, source_target_pairs={{0,2},{2,4},{4,6},{6,7},{7,5},{5,3},{3,1},{1,0},{8,10},{10,12},{12... | collective-permute-start | bytes 1179656 | tf_op jit(solution)/shard_map/ppermute | solution.py:50
  45.2 36.5 %collective-permute-start.16 = (bf16[512,384]{1,0:T(8,128)(2,1)}, bf16[512,384]{1,0:T(8,128)(2,1)S(1)}, u32[]{:S(2)}, u32[]{:S(2)}) collective-permute-start(bf16[512,384]{1,0:T(8,128)(2,1)} %collective-permute-done.15.refs_8_), channel_id=1, source_target_pairs={{2,0},{4,2},{6,4},{7,6},{5,7},{3,5},{1,3},{0,1},{10,8},{12,10},{14... | collective-permute-start | bytes 1179656 | tf_op jit(solution)/shard_map/ppermute | solution.py:50
  47.1 36.9 %collective-permute-start.3 = (bf16[512,384]{1,0:T(8,128)(2,1)S(1)}, bf16[512,384]{1,0:T(8,128)(2,1)S(1)}, u32[]{:S(2)}, u32[]{:S(2)}) collective-permute-start(bf16[512,384]{1,0:T(8,128)(2,1)S(1)} %collective-permute-done.2.refs_2_), channel_id=1, source_target_pairs={{0,2},{2,4},{4,6},{6,7},{7,5},{5,3},{3,1},{1,0},{8,10},{10,12},{12... | collective-permute-start | bytes 1179656 | tf_op jit(solution)/shard_map/ppermute | solution.py:50
  51.5 30.4 %collective-permute-start.19 = (bf16[512,384]{1,0:T(8,128)(2,1)}, bf16[512,384]{1,0:T(8,128)(2,1)S(1)}, u32[]{:S(2)}, u32[]{:S(2)}) collective-permute-start(bf16[512,384]{1,0:T(8,128)(2,1)} %collective-permute-done.10.refs_0_), channel_id=1, source_target_pairs={{0,2},{2,4},{4,6},{6,7},{7,5},{5,3},{3,1},{1,0},{8,10},{10,12},{12... | collective-permute-start | bytes 1179656 | tf_op jit(solution)/shard_map/ppermute | solution.py:50
  53.6 30.2 %collective-permute-start.20 = (bf16[512,384]{1,0:T(8,128)(2,1)}, bf16[512,384]{1,0:T(8,128)(2,1)S(1)}, u32[]{:S(2)}, u32[]{:S(2)}) collective-permute-start(bf16[512,384]{1,0:T(8,128)(2,1)} %collective-permute-done.12.refs_1_), channel_id=1, source_target_pairs={{2,0},{4,2},{6,4},{7,6},{5,7},{3,5},{1,3},{0,1},{10,8},{12,10},{14... | collective-permute-start | bytes 1179656 | tf_op jit(solution)/shard_map/ppermute | solution.py:50
  79.7 26.3 %collective-permute-start.6 = (bf16[512,384]{1,0:T(8,128)(2,1)S(1)}, bf16[512,384]{1,0:T(8,128)(2,1)S(1)}, u32[]{:S(2)}, u32[]{:S(2)}) collective-permute-start(bf16[512,384]{1,0:T(8,128)(2,1)S(1)} %collective-permute-done.5.refs_3_), channel_id=1, source_target_pairs={{2,0},{4,2},{6,4},{7,6},{5,7},{3,5},{1,3},{0,1},{10,8},{12,10},{14... | collective-permute-start | bytes 1179656 | tf_op jit(solution)/shard_map/ppermute | solution.py:50
  81.7 24.6 %collective-permute-start.25 = (bf16[512,384]{1,0:T(8,128)(2,1)S(1)}, bf16[512,384]{1,0:T(8,128)(2,1)S(1)}, u32[]{:S(2)}, u32[]{:S(2)}) collective-permute-start(bf16[512,384]{1,0:T(8,128)(2,1)S(1)} %collective-permute-done.14.refs_4_), channel_id=1, source_target_pairs={{0,2},{2,4},{4,6},{6,7},{7,5},{5,3},{3,1},{1,0},{8,10},{10,12},{12... | collective-permute-start | bytes 1179656 | tf_op jit(solution)/shard_map/ppermute | solution.py:50
  81.9 26.4 %collective-permute-start.26 = (bf16[512,384]{1,0:T(8,128)(2,1)S(1)}, bf16[512,384]{1,0:T(8,128)(2,1)S(1)}, u32[]{:S(2)}, u32[]{:S(2)}) collective-permute-start(bf16[512,384]{1,0:T(8,128)(2,1)S(1)} %collective-permute-done.16.refs_5_), channel_id=1, source_target_pairs={{2,0},{4,2},{6,4},{7,6},{5,7},{3,5},{1,3},{0,1},{10,8},{12,10},{14... | collective-permute-start | bytes 1179656 | tf_op jit(solution)/shard_map/ppermute | solution.py:50
  83.8 24.7 %collective-permute-start.21 = (bf16[256,384]{1,0:T(8,128)(2,1)S(1)}, bf16[256,384]{1,0:T(8,128)(2,1)S(1)}, u32[]{:S(2)}, u32[]{:S(2)}) collective-permute-start(bf16[256,384]{1,0:T(8,128)(2,1)S(1)} %slice.95), channel_id=1, source_target_pairs={{0,2},{2,4},{4,6},{6,7},{7,5},{5,3},{3,1},{1,0},{8,10},{10,12},{12... | collective-permute-start | bytes 589832 | tf_op jit(solution)/shard_map/ppermute | solution.py:50
  84.1 26.4 %collective-permute-start.22 = (bf16[256,384]{1,0:T(8,128)(2,1)S(1)}, bf16[256,384]{1,0:T(8,128)(2,1)S(1)}, u32[]{:S(2)}, u32[]{:S(2)}) collective-permute-start(bf16[256,384]{1,0:T(8,128)(2,1)S(1)} %slice.96), channel_id=1, source_target_pairs={{2,0},{4,2},{6,4},{7,6},{5,7},{3,5},{1,3},{0,1},{10,8},{12,10},{14... | collective-permute-start | bytes 589832 | tf_op jit(solution)/shard_map/ppermute | solution.py:50
  108.3 29.0 %collective-permute-start.27 = (bf16[256,384]{1,0:T(8,128)(2,1)S(1)}, bf16[256,384]{1,0:T(8,128)(2,1)S(1)}, u32[]{:S(2)}, u32[]{:S(2)}) collective-permute-start(bf16[256,384]{1,0:T(8,128)(2,1)S(1)} %slice.97), channel_id=1, source_target_pairs={{0,2},{2,4},{4,6},{6,7},{7,5},{5,3},{3,1},{1,0},{8,10},{10,12},{12... | collective-permute-start | bytes 589832 | tf_op jit(solution)/shard_map/ppermute | solution.py:50
  108.5 28.7 %collective-permute-start.28 = (bf16[256,384]{1,0:T(8,128)(2,1)S(1)}, bf16[256,384]{1,0:T(8,128)(2,1)S(1)}, u32[]{:S(2)}, u32[]{:S(2)}) collective-permute-start(bf16[256,384]{1,0:T(8,128)(2,1)S(1)} %slice.98), channel_id=1, source_target_pairs={{2,0},{4,2},{6,4},{7,6},{5,7},{3,5},{1,3},{0,1},{10,8},{12,10},{14... | collective-permute-start | bytes 589832 | tf_op jit(solution)/shard_map/ppermute | solution.py:50
  123.2 29.1 %collective-permute-start.23 = (f32[2,512,384]{2,1,0:T(8,128)}, f32[2,512,384]{2,1,0:T(8,128)}, u32[]{:S(2)}, u32[]{:S(2)}) collective-permute-start(f32[2,512,384]{2,1,0:T(8,128)} %get-tuple-element.69), channel_id=1, source_target_pairs={{0,8},{8,0},{16,24},{24,16},{1,9},{9,1},{17,25},{25,17},{2,10},{10... | collective-permute-start | bytes 4718600 | tf_op jit(solution)/shard_map/ppermute | solution.py:650
  136.8 23.2 %collective-permute-start.17 = (f32[2,512,384]{2,1,0:T(8,128)}, f32[2,512,384]{2,1,0:T(8,128)}, u32[]{:S(2)}, u32[]{:S(2)}) collective-permute-start(f32[2,512,384]{2,1,0:T(8,128)} %get-tuple-element.63), channel_id=1, source_target_pairs={{0,8},{8,0},{16,24},{24,16},{1,9},{9,1},{17,25},{25,17},{2,10},{10... | collective-permute-start | bytes 4718600 | tf_op jit(solution)/shard_map/ppermute | solution.py:650
  150.7 52.8 %collective-permute-start = (bf16[3,512,384]{2,1,0:T(8,128)(2,1)}, bf16[3,512,384]{2,1,0:T(8,128)(2,1)}, u32[]{:S(2)}, u32[]{:S(2)}) collective-permute-start(bf16[3,512,384]{2,1,0:T(8,128)(2,1)} %get-tuple-element.57), channel_id=1, source_target_pairs={{4,1},{8,2},{12,3},{16,4},{20,5},{24,6},{28,7},{1,8},{5,9},{9,10},... | collective-permute-start | bytes 3538952 | tf_op jit(solution)/shard_map/ppermute | solution.py:630
  156.5 33.9 %collective-permute-start.24 = (s16[528,384]{1,0:T(8,128)(2,1)}, s16[528,384]{1,0:T(8,128)(2,1)S(1)}, u32[]{:S(2)}, u32[]{:S(2)}) collective-permute-start(s16[528,384]{1,0:T(8,128)(2,1)} %get-tuple-element.71), channel_id=1, source_target_pairs={{0,16},{8,24},{16,0},{24,8},{1,17},{9,25},{17,1},{25,9},{2,18},{10... | collective-permute-start | bytes 1216520 | tf_op jit(solution)/shard_map/ppermute | solution.py:653
  164.0 35.1 %collective-permute-start.18 = (s16[528,384]{1,0:T(8,128)(2,1)}, s16[528,384]{1,0:T(8,128)(2,1)}, u32[]{:S(2)}, u32[]{:S(2)}) collective-permute-start(s16[528,384]{1,0:T(8,128)(2,1)} %get-tuple-element.65), channel_id=1, source_target_pairs={{0,16},{8,24},{16,0},{24,8},{1,17},{9,25},{17,1},{25,9},{2,18},{10... | collective-permute-start | bytes 1216520 | tf_op jit(solution)/shard_map/ppermute | solution.py:653
  167.4 48.3 %collective-permute-start.30 = (s16[528,384]{1,0:T(8,128)(2,1)S(1)}, s16[528,384]{1,0:T(8,128)(2,1)S(1)}, u32[]{:S(2)}, u32[]{:S(2)}) collective-permute-start(s16[528,384]{1,0:T(8,128)(2,1)S(1)} %get-tuple-element.83), channel_id=1, source_target_pairs={{0,16},{8,24},{16,0},{24,8},{1,17},{9,25},{17,1},{25,9},{2,18},{10... | collective-permute-start | bytes 1216520 | tf_op jit(solution)/shard_map/ppermute | solution.py:653
  232.5 43.0 %collective-permute-start.47 = (s16[528,384]{1,0:T(8,128)(2,1)}, s16[528,384]{1,0:T(8,128)(2,1)}, u32[]{:S(2)}, u32[]{:S(2)}) collective-permute-start(s16[528,384]{1,0:T(8,128)(2,1)} %copy-done.20), channel_id=1, source_target_pairs={{0,0},{1,8},{2,2},{3,10},{4,4},{5,12},{6,6},{7,14},{8,1},{9,9},{10... | collective-permute-start | bytes 1216520 | tf_op jit(solution)/shard_map/ppermute | solution.py:688
  251.5 20.7 %collective-permute-start.33 = (s16[400,512]{1,0:T(8,128)(2,1)S(1)}, s16[400,512]{1,0:T(8,128)(2,1)S(1)}, u32[]{:S(2)}, u32[]{:S(2)}) collective-permute-start(s16[400,512]{1,0:T(8,128)(2,1)S(1)} %get-tuple-element.94), channel_id=1, source_target_pairs={{0,16},{1,17},{2,18},{3,19},{4,20},{5,21},{6,22},{7,23},{8,24},{9,... | collective-permute-start | bytes 1228808 | tf_op jit(solution)/shard_map/ppermute | solution.py:730
  274.1 43.9 %collective-permute-start.43 = (s16[528,384]{1,0:T(8,128)(2,1)S(1)}, s16[528,384]{1,0:T(8,128)(2,1)S(1)}, u32[]{:S(2)}, u32[]{:S(2)}) collective-permute-start(s16[528,384]{1,0:T(8,128)(2,1)S(1)} %copy-done.19), channel_id=1, source_target_pairs={{0,0},{1,8},{2,2},{3,10},{4,4},{5,12},{6,6},{7,14},{8,1},{9,9},{10... | collective-permute-start | bytes 1216520 | tf_op jit(solution)/shard_map/ppermute | solution.py:688
  274.7 43.3 %collective-permute-start.45 = (s16[528,384]{1,0:T(8,128)(2,1)S(1)}, s16[528,384]{1,0:T(8,128)(2,1)S(1)}, u32[]{:S(2)}, u32[]{:S(2)}) collective-permute-start(s16[528,384]{1,0:T(8,128)(2,1)S(1)} %get-tuple-element.101), channel_id=1, source_target_pairs={{0,0},{1,8},{2,2},{3,10},{4,4},{5,12},{6,6},{7,14},{8,1},{9,9},{10... | collective-permute-start | bytes 1216520 | tf_op jit(solution)/shard_map/ppermute | solution.py:688
  275.5 43.3 %collective-permute-start.48 = (s16[528,384]{1,0:T(8,128)(2,1)}, s16[528,384]{1,0:T(8,128)(2,1)S(1)}, u32[]{:S(2)}, u32[]{:S(2)}) collective-permute-start(s16[528,384]{1,0:T(8,128)(2,1)} %collective-permute-done.47), channel_id=1, source_target_pairs={{0,0},{8,4},{2,8},{10,12},{4,16},{12,20},{6,24},{14,28},{1,1},{9,5... | collective-permute-start | bytes 1216520 | tf_op jit(solution)/shard_map/ppermute | solution.py:689
  313.5 37.8 %collective-permute-start.41 = (s16[4,112,512]{2,1,0:T(8,128)(2,1)S(1)}, s16[4,112,512]{2,1,0:T(8,128)(2,1)S(1)}, u32[]{:S(2)}, u32[]{:S(2)}) collective-permute-start(s16[4,112,512]{2,1,0:T(8,128)(2,1)S(1)} %shard_map.173.refs_0_), channel_id=1, source_target_pairs={{0,16},{1,17},{2,18},{3,19},{4,20},{5,21},{6,22},{7,23},{8,24},{9,... | collective-permute-start | bytes 1376264 | tf_op jit(solution)/shard_map/ppermute | solution.py:730
  313.6 37.7 %collective-permute-start.42 = (s16[4,112,512]{2,1,0:T(8,128)(2,1)S(1)}, s16[4,112,512]{2,1,0:T(8,128)(2,1)S(1)}, u32[]{:S(2)}, u32[]{:S(2)}) collective-permute-start(s16[4,112,512]{2,1,0:T(8,128)(2,1)S(1)} %shard_map.173.refs_0_), channel_id=1, source_target_pairs={{0,17},{1,16},{2,19},{3,18},{4,21},{5,20},{6,23},{7,22},{8,25},{9,... | collective-permute-start | bytes 1376264 | tf_op jit(solution)/shard_map/ppermute | solution.py:730
  318.0 33.4 %collective-permute-start.49 = (s16[4,112,512]{2,1,0:T(8,128)(2,1)S(1)}, s16[4,112,512]{2,1,0:T(8,128)(2,1)S(1)}, u32[]{:S(2)}, u32[]{:S(2)}) collective-permute-start(s16[4,112,512]{2,1,0:T(8,128)(2,1)S(1)} %shard_map.173.refs_0_), channel_id=1, source_target_pairs={{0,1},{1,0},{2,3},{3,2},{4,5},{5,4},{6,7},{7,6},{8,9},{9,8},{10,11... | collective-permute-start | bytes 1376264 | tf_op jit(solution)/shard_map/ppermute | solution.py:730
  324.7 27.5 %collective-permute-start.50 = (s16[4,112,512]{2,1,0:T(8,128)(2,1)S(1)}, s16[4,112,512]{2,1,0:T(8,128)(2,1)S(1)}, u32[]{:S(2)}, u32[]{:S(2)}) collective-permute-start(s16[4,112,512]{2,1,0:T(8,128)(2,1)S(1)} %shard_map.173.refs_0_), channel_id=1, source_target_pairs={{0,8},{8,0},{16,24},{24,16},{1,9},{9,1},{17,25},{25,17},{2,10},{10... | collective-permute-start | bytes 1376264 | tf_op jit(solution)/shard_map/ppermute | solution.py:747
  (70 other events, 822.2 us)
where the time goes:
time: 371 us; the launch traced here: 366 us
  Pallas kernels  138 us (37%)
  starting transfers between devices  95.8 us (26%)
  waiting for transfers between devices  84.5 us (23%)
  local copies, waits for them, and re-layouts  19.1 us (5%)
  matrix products  17.9 us (5%)
  other arithmetic  9.25 us (2%)
    pallas_call x5, Pallas kernels, product_call(): pl.pallas_call(body, grid_spec=pltpu.PrefetchScalarGridSpec(num_scalar_pr...  82.3 us
    pallas_call x16, Pallas kernels, simple_call(): pl.pallas_call(body, grid_spec=pltpu.PrefetchScalarGridSpec(num_scalar_pr...  56 us
    ppermute x12, waiting for transfers between devices, exchange(): lax.ppermute(array, both, moves)  38.5 us
    ppermute x3, waiting for transfers between devices, lane_sums(): lax.ppermute(part, 'row', moves)  27.8 us
    ppermute x4, starting transfers between devices, local(): piles += [lax.ppermute(pile, 'row', sibling) for pile in piles]  26.3 us
    ppermute x12, starting transfers between devices, exchange(): lax.ppermute(array, both, moves)  21.3 us
    ppermute x12, starting transfers between devices, ring_step(): lax.ppermute(down, 'col', moves[1])  17.5 us
    ppermute x12, waiting for transfers between devices, ring_step(): lax.ppermute(up, 'col', moves[0])  15.7 us
  transfers between devices with their start and end apart: 54, of which 17 were waited for; matrix products, arithmetic and copies ran while one was open for 10% of the time, Pallas kernels for 30%

commit v1 on v0

--- a/solution.py
+++ b/solution.py
@@ -110,7 +110,7 @@
 
 def final_body(count, lanes, out_piece, sources, core, *refs):
     pieces = refs[: count + 1]
-    block, start, given, kept, total, doubled, terms = refs[count + 1 :]
+    block, start, given, kept, total, doubled = refs[count + 1 :]
     step = pl.program_id(0)
     for at in range(count - 1):
 
@@ -124,8 +124,9 @@
         put_double(doubled, pieces[count - 1], slice(0, half))
         put_double(doubled, pieces[count], slice(half, 2 * half))
 
-    terms[...] = two_terms(block)
-    add_product(doubled, terms, total, step == 0, start)
+    part = jnp.dot(doubled[...], two_terms(block), preferred_element_type=jnp.float32)
+
+    total[...] = jnp.where(step == 0, start[...], total[...]) + part
 
     @pl.when(step == count - 1)
     def _():
@@ -202,11 +203,7 @@
     return product_call(
         functools.partial(final_body, count, lanes, out_piece), (count,), 2,
         [sources, core, *pieces, block, start], in_specs, [half, half], [half_spec, half_spec],
-        [
-            pltpu.VMEM((width, cols), jnp.float32),
-            pltpu.VMEM((width, 2 * piece), jnp.bfloat16),
-            pltpu.VMEM((2 * piece, cols), jnp.bfloat16),
-        ],
+        [pltpu.VMEM((width, cols), jnp.float32), pltpu.VMEM((width, 2 * piece), jnp.bfloat16)],
         4 * count * width * piece * cols,
     )
 

time: 371 us -> 366 us (0.987)
  Pallas kernels: 138 us -> 133 us
    pallas_call x5, Pallas kernels: 82.3 us -> 76.9 us  [product_call(): pl.pallas_call(body, grid_spec=pltpu.PrefetchScalarGridSpec(num_scalar_pr...]
  transfers between devices with their start and end apart: 54 -> 54, of which waited for: 17 -> 17; matrix products, arithmetic and copies ran while one was open for 10% -> 10% of each run, Pallas kernels for 30% -> 29%
where the time goes in v1:
time: 366 us; the launch traced here: 361 us
  Pallas kernels  133 us (36%)
  starting transfers between devices  96.1 us (26%)
  waiting for transfers between devices  84.5 us (23%)
  local copies, waits for them, and re-layouts  19.1 us (5%)
  matrix products  17.8 us (5%)
  other arithmetic  9.25 us (3%)
    pallas_call x5, Pallas kernels, product_call(): pl.pallas_call(body, grid_spec=pltpu.PrefetchScalarGridSpec(num_scalar_pr...  76.9 us
    pallas_call x16, Pallas kernels, simple_call(): pl.pallas_call(body, grid_spec=pltpu.PrefetchScalarGridSpec(num_scalar_pr...  56 us
    ppermute x12, waiting for transfers between devices, exchange(): lax.ppermute(array, both, moves)  38.5 us
    ppermute x3, waiting for transfers between devices, lane_sums(): lax.ppermute(part, 'row', moves)  27.7 us
    ppermute x4, starting transfers between devices, local(): piles += [lax.ppermute(pile, 'row', sibling) for pile in piles]  26.3 us
    ppermute x12, starting transfers between devices, exchange(): lax.ppermute(array, both, moves)  21.3 us
    ppermute x12, starting transfers between devices, ring_step(): lax.ppermute(down, 'col', moves[1])  17.7 us
    ppermute x12, waiting for transfers between devices, ring_step(): lax.ppermute(up, 'col', moves[0])  15.7 us
  transfers between devices with their start and end apart: 54, of which 17 were waited for; matrix products, arithmetic and copies ran while one was open for 10% of the time, Pallas kernels for 29%

profile of v1, /device:TPU:0, one launch (start us, length us, event | category | flops | bytes accessed | tf_op | source)
XLA Modules:
  0.0 360.9 jit_solution(4085577732564803435)
XLA Ops:
  4.7 3.1 collective-permute-start.1
  21.4 4.7 %collective-permute-done.9.refs_1_ = bf16[512,384]{1,0:T(8,128)(2,1)} collective-permute-done((bf16[512,384]{1,0:T(8,128)(2,1)S(1)}, bf16[512,384]{1,0:T(8,128)(2,1)}, u32[]{:S(2)}, u32[]{:S(2)}) %collective-permute-start.9) | collective-permute-done | bytes 393248 | tf_op jit(solution)/shard_map/ppermute | solution.py:50
  29.9 4.6 %collective-permute-done.13.refs_7_ = bf16[512,384]{1,0:T(8,128)(2,1)S(1)} collective-permute-done((bf16[512,384]{1,0:T(8,128)(2,1)S(1)}, bf16[512,384]{1,0:T(8,128)(2,1)S(1)}, u32[]{:S(2)}, u32[]{:S(2)}) %collective-permute-start.13) | collective-permute-done | bytes 393248 | tf_op jit(solution)/shard_map/ppermute | solution.py:50
  37.8 3.5 copy.26
  41.3 3.7 %fusion = (bf16[3,512,512]{2,1,0:T(8,128)(2,1)}, bf16[3,512,512]{2,1,0:T(8,128)(2,1)S(1)}) fusion(f32[3,512,512]{1,2,0:T(8,128)} %copy.26), kind=kLoop, calls=%fused_computation.6 | loop fusion | flops 3145728 | bytes 6291456 | tf_op jit(solution)/shard_map/convert_element_type | solution.py:28
  47.3 4.2 %collective-permute-done.10.refs_0_ = bf16[512,384]{1,0:T(8,128)(2,1)} collective-permute-done((bf16[512,384]{1,0:T(8,128)(2,1)}, bf16[512,384]{1,0:T(8,128)(2,1)}, u32[]{:S(2)}, u32[]{:S(2)}) %collective-permute-start.10) | collective-permute-done | bytes 393248 | tf_op jit(solution)/shard_map/ppermute | solution.py:50
  53.6 26.1 %shard_map.158.refs_7_ = f32[3,512,1536]{2,1,0:T(8,128)} custom-call(s32[3]{0:T(128)} %get-tuple-element.115.sources, bf16[512,384]{1,0:T(8,128)(2,1)} %copy-done.4, bf16[512,384]{1,0:T(8,128)(2,1)} %collective-permute-done.9.refs_1_, bf16[512,384]{1,0:T(8,128)(2,1)} %collective-permute-done.11.refs_2_, bf16[512,384]{1,0:T(8,128)(2,1)} %copy-done.11, ...), custom_call_target="tpu_custom_call" | custom-call | flops 10871635968 | bytes 21233664 | tf_op jit(solution)/shard_map/pallas_call | solution.py:147
  86.0 20.0 %shard_map.159.refs_5_ = f32[3,512,1536]{2,1,0:T(8,128)} custom-call(s32[2]{0:T(128)} %slice.73.sources, bf16[512,384]{1,0:T(8,128)(2,1)} %collective-permute-done.10.refs_0_, bf16[512,384]{1,0:T(8,128)(2,1)} %collective-permute-done.12.refs_1_, bf16[512,384]{1,0:T(8,128)(2,1)} %copy-done.35, ...), custom_call_target="tpu_custom_call", output_to_operand_aliasing={{}: (8, {})} | custom-call | flops 7247757312 | bytes 14155776 | tf_op jit(solution)/shard_map/pallas_call | solution.py:147
  111.3 10.3 %shard_map.162 = (f32[2,512,384]{2,1,0:T(8,128)}, f32[2,512,384]{2,1,0:T(8,128)}) custom-call(s32[3]{0:T(128)} %get-tuple-element.116.sources, s32[1]{0:T(128)} %bitcast.3.core, bf16[512,384]{1,0:T(8,128)(2,1)} %copy-done.32, bf16[512,384]{1,0:T(8,128)(2,1)} %copy-done.34, bf16[256,384]{1,0:T(8,128)(2,1)} %copy-done.39, bf16[256,384]{1,0:T(8,128)(2,1)} %copy-done.42, ...), custom_call_target="tpu_custom_call" | custom-call | flops 3623878656 | bytes 7077888 | tf_op jit(solution)/shard_map/pallas_call | solution.py:147
  123.0 10.3 %shard_map.160 = (f32[2,512,384]{2,1,0:T(8,128)}, f32[2,512,384]{2,1,0:T(8,128)}) custom-call(s32[3]{0:T(128)} %get-tuple-element.116.sources, s32[1]{0:T(128)} %bitcast.3.core, bf16[512,384]{1,0:T(8,128)(2,1)} %copy-done.29, bf16[512,384]{1,0:T(8,128)(2,1)} %copy-done.33, bf16[256,384]{1,0:T(8,128)(2,1)} %copy-done.41, bf16[256,384]{1,0:T(8,128)(2,1)} %copy-done.44, ...), custom_call_target="tpu_custom_call" | custom-call | flops 3623878656 | bytes 7077888 | tf_op jit(solution)/shard_map/pallas_call | solution.py:147
  135.1 10.3 %shard_map.166 = (f32[2,512,384]{2,1,0:T(8,128)}, f32[2,512,384]{2,1,0:T(8,128)}) custom-call(s32[3]{0:T(128)} %get-tuple-element.116.sources, s32[1]{0:T(128)} %bitcast.3.core, bf16[512,384]{1,0:T(8,128)(2,1)} %copy-done.30, bf16[512,384]{1,0:T(8,128)(2,1)} %copy-done.31, bf16[256,384]{1,0:T(8,128)(2,1)} %copy-done.40, bf16[256,384]{1,0:T(8,128)(2,1)} %copy-done.43, ...), custom_call_target="tpu_custom_call" | custom-call | flops 3623878656 | bytes 7077888 | tf_op jit(solution)/shard_map/pallas_call | solution.py:147
  147.1 3.2 shard_map.163
  151.2 3.5 collective-permute-start.24
  154.7 3.2 shard_map.161
  164.2 20.9 %collective-permute-done.24.refs_1_ = s16[528,384]{1,0:T(8,128)(2,1)S(1)} collective-permute-done((s16[528,384]{1,0:T(8,128)(2,1)}, s16[528,384]{1,0:T(8,128)(2,1)S(1)}, u32[]{:S(2)}, u32[]{:S(2)}) %collective-permute-start.24) | collective-permute-done | bytes 405536 | tf_op jit(solution)/shard_map/ppermute | solution.py:650
  187.0 6.8 %collective-permute-done.18.refs_1_ = s16[528,384]{1,0:T(8,128)(2,1)} collective-permute-done((s16[528,384]{1,0:T(8,128)(2,1)}, s16[528,384]{1,0:T(8,128)(2,1)}, u32[]{:S(2)}, u32[]{:S(2)}) %collective-permute-start.18) | collective-permute-done | bytes 405536 | tf_op jit(solution)/shard_map/ppermute | solution.py:650
  193.8 4.4 %shard_map.165 = (f32[512,384]{1,0:T(8,128)S(1)}, s16[528,384]{1,0:T(8,128)(2,1)S(1)}, f32[3,384,512]{2,1,0:T(8,128)}) custom-call(f32[512,384]{1,0:T(8,128)S(1)} %copy-done.10, s16[528,384]{1,0:T(8,128)(2,1)} %collective-permute-done.18.refs_1_, bf16[3,512,512]{2,1,0:T(8,128)(2,1)S(1)} %get-tuple-element.66.refs_2_.refs_3_, ...), custom_call_target="tpu_custom_call", output_to_operand_aliasing={{2}: (5, {})} | custom-call | flops 7483392 | bytes 7483392 | tf_op jit(solution)/shard_map/pallas_call | solution.py:242
  210.4 5.4 %shard_map.168 = (f32[512,384]{1,0:T(8,128)}, s16[528,384]{1,0:T(8,128)(2,1)S(1)}, f32[3,384,512]{2,1,0:T(8,128)}) custom-call(f32[512,384]{1,0:T(8,128)S(1)} %get-tuple-element.82.refs_0_, s16[528,384]{1,0:T(8,128)(2,1)S(1)} %collective-permute-done.30.refs_1_, ...), custom_call_target="tpu_custom_call", output_to_operand_aliasing={{2}: (8, {})} | custom-call | flops 11415552 | bytes 11415552 | tf_op jit(solution)/shard_map/pallas_call | solution.py:242
  217.6 9.6 %shard_map.169 = (f32[3,512,512]{2,1,0:T(8,128)S(1)}, f32[3,512,512]{2,1,0:T(8,128)}) custom-call(s32[6]{0:T(128)S(1)} %get-tuple-element.124.low, s32[6]{0:T(128)S(1)} %get-tuple-element.123.up, bf16[3,512,1152]{2,1,0:T(8,128)(2,1)} %pad_maximum_fusion.left, f32[3,384,512]{2,1,0:T(8,128)S(1)} %copy-done), custom_call_target="tpu_custom_call" | custom-call | flops 5898288 | bytes 5898288 | tf_op jit(solution)/shard_map/pallas_call | solution.py:242
  227.2 4.9 %collective-permute-start.47 = (s16[528,384]{1,0:T(8,128)(2,1)}, s16[528,384]{1,0:T(8,128)(2,1)}, u32[]{:S(2)}, u32[]{:S(2)}) collective-permute-start(s16[528,384]{1,0:T(8,128)(2,1)} %copy-done.20), channel_id=1, source_target_pairs={{0,0},{1,8},{2,2},{3,10},{4,4},{5,12},{6,6},{7,14},{8,1},{9,9},{10... | collective-permute-start | bytes 1216520 | tf_op jit(solution)/shard_map/ppermute | solution.py:685
  234.4 4.4 %shard_map.170 = (f32[384,512]{1,0:T(8,128)S(1)}, s16[400,512]{1,0:T(8,128)(2,1)S(1)}, s16[400,512]{1,0:T(8,128)(2,1)S(1)}, s16[400,512]{1,0:T(8,128)(2,1)S(1)}) custom-call(s32[4]{0:T(128)S(1)} %fusion.35.starts, f32[1536,512]{1,0:T(8,128)S(1)} %bitcast.93, f32[1536,512]{1,0:T(8,128)} %collective-permute-done.31.refs_1_), custom_call_target="tpu_custom_call" | custom-call | flops 6291472 | bytes 6291472 | tf_op jit(solution)/shard_map/pallas_call | solution.py:242
  241.1 5.2 %collective-permute-start.32 = (s16[400,512]{1,0:T(8,128)(2,1)S(1)}, s16[400,512]{1,0:T(8,128)(2,1)S(1)}, u32[]{:S(2)}, u32[]{:S(2)}) collective-permute-start(s16[400,512]{1,0:T(8,128)(2,1)S(1)} %get-tuple-element.93), channel_id=1, source_target_pairs={{0,1},{1,0},{2,3},{3,2},{4,5},{5,4},{6,7},{7,6},{8,9},{9,8},{10,11... | collective-permute-start | bytes 1228808 | tf_op jit(solution)/shard_map/ppermute | solution.py:727
  255.6 11.4 %collective-permute-done.33.refs_2_ = s16[400,512]{1,0:T(8,128)(2,1)S(1)} collective-permute-done((s16[400,512]{1,0:T(8,128)(2,1)S(1)}, s16[400,512]{1,0:T(8,128)(2,1)S(1)}, u32[]{:S(2)}, u32[]{:S(2)}) %collective-permute-start.33) | collective-permute-done | bytes 409632 | tf_op jit(solution)/shard_map/ppermute | solution.py:727
  271.9 3.1 collective-permute-start.36
  274.9 5.6 %collective-permute-start.37 = (s16[112,512]{1,0:T(8,128)(2,1)S(1)}, s16[112,512]{1,0:T(8,128)(2,1)S(1)}, u32[]{:S(2)}, u32[]{:S(2)}) collective-permute-start(s16[112,512]{1,0:T(8,128)(2,1)S(1)} %get-tuple-element.99), channel_id=1, source_target_pairs={{0,6},{1,7},{2,4},{3,5},{4,2},{5,3},{6,0},{7,1},{8,14},{9,15},{10,... | collective-permute-start | bytes 344072 | tf_op jit(solution)/shard_map/ppermute | solution.py:727
  280.5 6.9 %collective-permute-done.36.refs_2_ = s16[112,512]{1,0:T(8,128)(2,1)S(1)} collective-permute-done((s16[112,512]{1,0:T(8,128)(2,1)S(1)}, s16[112,512]{1,0:T(8,128)(2,1)S(1)}, u32[]{:S(2)}, u32[]{:S(2)}) %collective-permute-start.36) | collective-permute-done | bytes 114720 | tf_op jit(solution)/shard_map/ppermute | solution.py:727
  287.4 7.1 %collective-permute-done.37.refs_3_ = s16[112,512]{1,0:T(8,128)(2,1)S(1)} collective-permute-done((s16[112,512]{1,0:T(8,128)(2,1)S(1)}, s16[112,512]{1,0:T(8,128)(2,1)S(1)}, u32[]{:S(2)}, u32[]{:S(2)}) %collective-permute-start.37) | collective-permute-done | bytes 114720 | tf_op jit(solution)/shard_map/ppermute | solution.py:727
  296.2 3.7 %collective-permute-done.38.refs_1_ = s16[112,512]{1,0:T(8,128)(2,1)S(1)} collective-permute-done((s16[112,512]{1,0:T(8,128)(2,1)S(1)}, s16[112,512]{1,0:T(8,128)(2,1)S(1)}, u32[]{:S(2)}, u32[]{:S(2)}) %collective-permute-start.38) | collective-permute-done | bytes 114720 | tf_op jit(solution)/shard_map/ppermute | solution.py:727
  299.9 8.0 %collective-permute-done.39.refs_2_ = s16[112,512]{1,0:T(8,128)(2,1)S(1)} collective-permute-done((s16[112,512]{1,0:T(8,128)(2,1)S(1)}, s16[112,512]{1,0:T(8,128)(2,1)S(1)}, u32[]{:S(2)}, u32[]{:S(2)}) %collective-permute-start.39) | collective-permute-done | bytes 114720 | tf_op jit(solution)/shard_map/ppermute | solution.py:727
  308.4 4.4 %collective-permute-start.42 = (s16[4,112,512]{2,1,0:T(8,128)(2,1)S(1)}, s16[4,112,512]{2,1,0:T(8,128)(2,1)S(1)}, u32[]{:S(2)}, u32[]{:S(2)}) collective-permute-start(s16[4,112,512]{2,1,0:T(8,128)(2,1)S(1)} %shard_map.173.refs_0_), channel_id=1, source_target_pairs={{0,17},{1,16},{2,19},{3,18},{4,21},{5,20},{6,23},{7,22},{8,25},{9,... | collective-permute-start | bytes 1376264 | tf_op jit(solution)/shard_map/ppermute | solution.py:727
  319.5 25.7 %collective-permute-start.50 = (s16[4,112,512]{2,1,0:T(8,128)(2,1)S(1)}, s16[4,112,512]{2,1,0:T(8,128)(2,1)S(1)}, u32[]{:S(2)}, u32[]{:S(2)}) collective-permute-start(s16[4,112,512]{2,1,0:T(8,128)(2,1)S(1)} %shard_map.173.refs_0_), channel_id=1, source_target_pairs={{0,8},{8,0},{16,24},{24,16},{1,9},{9,1},{17,25},{25,17},{2,10},{10... | collective-permute-start | bytes 1376264 | tf_op jit(solution)/shard_map/ppermute | solution.py:744
  349.4 11.6 %shard_map.177 = f32[3,3,512,512]{3,2,1,0:T(8,128)} custom-call(s32[32]{0:T(128)S(1)} %pad_add_fusion.place, s32[9]{0:T(128)S(1)} %copy-done.16, s32[9]{0:T(128)S(1)} %copy-done.17, s16[4,112,512]{2,1,0:T(8,128)(2,1)S(1)} %shard_map.173.refs_0_, s16[4,112,512]{2,1,0:T(8,128)(2,1)S(1)} %collective-permute-done.49.refs_1_, ...), custom_call_target="tpu_custom_call" | custom-call | flops 9961672 | bytes 9961672 | tf_op jit(solution)/shard_map/pallas_call | solution.py:242
  (231 shorter events, 99.9 us)
Async XLA Ops:
  9.8 24.7 %collective-permute-start.13 = (bf16[512,384]{1,0:T(8,128)(2,1)S(1)}, bf16[512,384]{1,0:T(8,128)(2,1)S(1)}, u32[]{:S(2)}, u32[]{:S(2)}) collective-permute-start(bf16[512,384]{1,0:T(8,128)(2,1)S(1)} %get-tuple-element.59.refs_6_), channel_id=1, source_target_pairs={{0,2},{2,4},{4,6},{6,7},{7,5},{5,3},{3,1},{1,0},{8,10},{10,12},{12... | collective-permute-start | bytes 1179656 | tf_op jit(solution)/shard_map/ppermute | solution.py:50
  17.8 27.3 %collective-permute-start.15 = (bf16[512,384]{1,0:T(8,128)(2,1)S(1)}, bf16[512,384]{1,0:T(8,128)(2,1)}, u32[]{:S(2)}, u32[]{:S(2)}) collective-permute-start(bf16[512,384]{1,0:T(8,128)(2,1)S(1)} %get-tuple-element.59.refs_6_), channel_id=1, source_target_pairs={{2,0},{4,2},{6,4},{7,6},{5,7},{3,5},{1,3},{0,1},{10,8},{12,10},{14... | collective-permute-start | bytes 1179656 | tf_op jit(solution)/shard_map/ppermute | solution.py:50
  19.9 25.3 %collective-permute-start.2 = (bf16[512,384]{1,0:T(8,128)(2,1)}, bf16[512,384]{1,0:T(8,128)(2,1)S(1)}, u32[]{:S(2)}, u32[]{:S(2)}) collective-permute-start(bf16[512,384]{1,0:T(8,128)(2,1)} %collective-permute-done.1.refs_4_), channel_id=1, source_target_pairs={{0,2},{2,4},{4,6},{6,7},{7,5},{5,3},{3,1},{1,0},{8,10},{10,12},{12... | collective-permute-start | bytes 1179656 | tf_op jit(solution)/shard_map/ppermute | solution.py:50
  26.2 20.9 %collective-permute-start.5 = (bf16[512,384]{1,0:T(8,128)(2,1)}, bf16[512,384]{1,0:T(8,128)(2,1)S(1)}, u32[]{:S(2)}, u32[]{:S(2)}) collective-permute-start(bf16[512,384]{1,0:T(8,128)(2,1)} %collective-permute-done.4.refs_5_), channel_id=1, source_target_pairs={{2,0},{4,2},{6,4},{7,6},{5,7},{3,5},{1,3},{0,1},{10,8},{12,10},{14... | collective-permute-start | bytes 1179656 | tf_op jit(solution)/shard_map/ppermute | solution.py:50
  28.3 23.2 %collective-permute-start.10 = (bf16[512,384]{1,0:T(8,128)(2,1)}, bf16[512,384]{1,0:T(8,128)(2,1)}, u32[]{:S(2)}, u32[]{:S(2)}) collective-permute-start(bf16[512,384]{1,0:T(8,128)(2,1)} %collective-permute-done.9.refs_1_), channel_id=1, source_target_pairs={{0,2},{2,4},{4,6},{6,7},{7,5},{5,3},{3,1},{1,0},{8,10},{10,12},{12... | collective-permute-start | bytes 1179656 | tf_op jit(solution)/shard_map/ppermute | solution.py:50
  45.1 34.6 %collective-permute-start.14 = (bf16[512,384]{1,0:T(8,128)(2,1)S(1)}, bf16[512,384]{1,0:T(8,128)(2,1)S(1)}, u32[]{:S(2)}, u32[]{:S(2)}) collective-permute-start(bf16[512,384]{1,0:T(8,128)(2,1)S(1)} %copy-done.47), channel_id=1, source_target_pairs={{0,2},{2,4},{4,6},{6,7},{7,5},{5,3},{3,1},{1,0},{8,10},{10,12},{12... | collective-permute-start | bytes 1179656 | tf_op jit(solution)/shard_map/ppermute | solution.py:50
  45.2 36.5 %collective-permute-start.16 = (bf16[512,384]{1,0:T(8,128)(2,1)}, bf16[512,384]{1,0:T(8,128)(2,1)S(1)}, u32[]{:S(2)}, u32[]{:S(2)}) collective-permute-start(bf16[512,384]{1,0:T(8,128)(2,1)} %collective-permute-done.15.refs_8_), channel_id=1, source_target_pairs={{2,0},{4,2},{6,4},{7,6},{5,7},{3,5},{1,3},{0,1},{10,8},{12,10},{14... | collective-permute-start | bytes 1179656 | tf_op jit(solution)/shard_map/ppermute | solution.py:50
  47.1 36.9 %collective-permute-start.3 = (bf16[512,384]{1,0:T(8,128)(2,1)S(1)}, bf16[512,384]{1,0:T(8,128)(2,1)S(1)}, u32[]{:S(2)}, u32[]{:S(2)}) collective-permute-start(bf16[512,384]{1,0:T(8,128)(2,1)S(1)} %collective-permute-done.2.refs_2_), channel_id=1, source_target_pairs={{0,2},{2,4},{4,6},{6,7},{7,5},{5,3},{3,1},{1,0},{8,10},{10,12},{12... | collective-permute-start | bytes 1179656 | tf_op jit(solution)/shard_map/ppermute | solution.py:50
  51.5 30.4 %collective-permute-start.19 = (bf16[512,384]{1,0:T(8,128)(2,1)}, bf16[512,384]{1,0:T(8,128)(2,1)S(1)}, u32[]{:S(2)}, u32[]{:S(2)}) collective-permute-start(bf16[512,384]{1,0:T(8,128)(2,1)} %collective-permute-done.10.refs_0_), channel_id=1, source_target_pairs={{0,2},{2,4},{4,6},{6,7},{7,5},{5,3},{3,1},{1,0},{8,10},{10,12},{12... | collective-permute-start | bytes 1179656 | tf_op jit(solution)/shard_map/ppermute | solution.py:50
  53.6 30.2 %collective-permute-start.20 = (bf16[512,384]{1,0:T(8,128)(2,1)}, bf16[512,384]{1,0:T(8,128)(2,1)S(1)}, u32[]{:S(2)}, u32[]{:S(2)}) collective-permute-start(bf16[512,384]{1,0:T(8,128)(2,1)} %collective-permute-done.12.refs_1_), channel_id=1, source_target_pairs={{2,0},{4,2},{6,4},{7,6},{5,7},{3,5},{1,3},{0,1},{10,8},{12,10},{14... | collective-permute-start | bytes 1179656 | tf_op jit(solution)/shard_map/ppermute | solution.py:50
  79.7 26.3 %collective-permute-start.6 = (bf16[512,384]{1,0:T(8,128)(2,1)S(1)}, bf16[512,384]{1,0:T(8,128)(2,1)S(1)}, u32[]{:S(2)}, u32[]{:S(2)}) collective-permute-start(bf16[512,384]{1,0:T(8,128)(2,1)S(1)} %collective-permute-done.5.refs_3_), channel_id=1, source_target_pairs={{2,0},{4,2},{6,4},{7,6},{5,7},{3,5},{1,3},{0,1},{10,8},{12,10},{14... | collective-permute-start | bytes 1179656 | tf_op jit(solution)/shard_map/ppermute | solution.py:50
  81.7 24.6 %collective-permute-start.25 = (bf16[512,384]{1,0:T(8,128)(2,1)S(1)}, bf16[512,384]{1,0:T(8,128)(2,1)S(1)}, u32[]{:S(2)}, u32[]{:S(2)}) collective-permute-start(bf16[512,384]{1,0:T(8,128)(2,1)S(1)} %collective-permute-done.14.refs_4_), channel_id=1, source_target_pairs={{0,2},{2,4},{4,6},{6,7},{7,5},{5,3},{3,1},{1,0},{8,10},{10,12},{12... | collective-permute-start | bytes 1179656 | tf_op jit(solution)/shard_map/ppermute | solution.py:50
  81.9 26.4 %collective-permute-start.26 = (bf16[512,384]{1,0:T(8,128)(2,1)S(1)}, bf16[512,384]{1,0:T(8,128)(2,1)S(1)}, u32[]{:S(2)}, u32[]{:S(2)}) collective-permute-start(bf16[512,384]{1,0:T(8,128)(2,1)S(1)} %collective-permute-done.16.refs_5_), channel_id=1, source_target_pairs={{2,0},{4,2},{6,4},{7,6},{5,7},{3,5},{1,3},{0,1},{10,8},{12,10},{14... | collective-permute-start | bytes 1179656 | tf_op jit(solution)/shard_map/ppermute | solution.py:50
  83.8 24.7 %collective-permute-start.21 = (bf16[256,384]{1,0:T(8,128)(2,1)S(1)}, bf16[256,384]{1,0:T(8,128)(2,1)S(1)}, u32[]{:S(2)}, u32[]{:S(2)}) collective-permute-start(bf16[256,384]{1,0:T(8,128)(2,1)S(1)} %slice.95), channel_id=1, source_target_pairs={{0,2},{2,4},{4,6},{6,7},{7,5},{5,3},{3,1},{1,0},{8,10},{10,12},{12... | collective-permute-start | bytes 589832 | tf_op jit(solution)/shard_map/ppermute | solution.py:50
  84.1 26.6 %collective-permute-start.22 = (bf16[256,384]{1,0:T(8,128)(2,1)S(1)}, bf16[256,384]{1,0:T(8,128)(2,1)S(1)}, u32[]{:S(2)}, u32[]{:S(2)}) collective-permute-start(bf16[256,384]{1,0:T(8,128)(2,1)S(1)} %slice.96), channel_id=1, source_target_pairs={{2,0},{4,2},{6,4},{7,6},{5,7},{3,5},{1,3},{0,1},{10,8},{12,10},{14... | collective-permute-start | bytes 589832 | tf_op jit(solution)/shard_map/ppermute | solution.py:50
  108.3 25.5 %collective-permute-start.27 = (bf16[256,384]{1,0:T(8,128)(2,1)S(1)}, bf16[256,384]{1,0:T(8,128)(2,1)S(1)}, u32[]{:S(2)}, u32[]{:S(2)}) collective-permute-start(bf16[256,384]{1,0:T(8,128)(2,1)S(1)} %slice.97), channel_id=1, source_target_pairs={{0,2},{2,4},{4,6},{6,7},{7,5},{5,3},{3,1},{1,0},{8,10},{10,12},{12... | collective-permute-start | bytes 589832 | tf_op jit(solution)/shard_map/ppermute | solution.py:50
  108.5 25.3 %collective-permute-start.28 = (bf16[256,384]{1,0:T(8,128)(2,1)S(1)}, bf16[256,384]{1,0:T(8,128)(2,1)S(1)}, u32[]{:S(2)}, u32[]{:S(2)}) collective-permute-start(bf16[256,384]{1,0:T(8,128)(2,1)S(1)} %slice.98), channel_id=1, source_target_pairs={{2,0},{4,2},{6,4},{7,6},{5,7},{3,5},{1,3},{0,1},{10,8},{12,10},{14... | collective-permute-start | bytes 589832 | tf_op jit(solution)/shard_map/ppermute | solution.py:50
  121.6 25.5 %collective-permute-start.23 = (f32[2,512,384]{2,1,0:T(8,128)}, f32[2,512,384]{2,1,0:T(8,128)}, u32[]{:S(2)}, u32[]{:S(2)}) collective-permute-start(f32[2,512,384]{2,1,0:T(8,128)} %get-tuple-element.69), channel_id=1, source_target_pairs={{0,8},{8,0},{16,24},{24,16},{1,9},{9,1},{17,25},{25,17},{2,10},{10... | collective-permute-start | bytes 4718600 | tf_op jit(solution)/shard_map/ppermute | solution.py:647
  133.3 21.4 %collective-permute-start.17 = (f32[2,512,384]{2,1,0:T(8,128)}, f32[2,512,384]{2,1,0:T(8,128)}, u32[]{:S(2)}, u32[]{:S(2)}) collective-permute-start(f32[2,512,384]{2,1,0:T(8,128)} %get-tuple-element.63), channel_id=1, source_target_pairs={{0,8},{8,0},{16,24},{24,16},{1,9},{9,1},{17,25},{25,17},{2,10},{10... | collective-permute-start | bytes 4718600 | tf_op jit(solution)/shard_map/ppermute | solution.py:647
  145.4 52.8 %collective-permute-start = (bf16[3,512,384]{2,1,0:T(8,128)(2,1)}, bf16[3,512,384]{2,1,0:T(8,128)(2,1)}, u32[]{:S(2)}, u32[]{:S(2)}) collective-permute-start(bf16[3,512,384]{2,1,0:T(8,128)(2,1)} %get-tuple-element.57), channel_id=1, source_target_pairs={{4,1},{8,2},{12,3},{16,4},{20,5},{24,6},{28,7},{1,8},{5,9},{9,10},... | collective-permute-start | bytes 3538952 | tf_op jit(solution)/shard_map/ppermute | solution.py:627
  151.2 33.9 %collective-permute-start.24 = (s16[528,384]{1,0:T(8,128)(2,1)}, s16[528,384]{1,0:T(8,128)(2,1)S(1)}, u32[]{:S(2)}, u32[]{:S(2)}) collective-permute-start(s16[528,384]{1,0:T(8,128)(2,1)} %get-tuple-element.71), channel_id=1, source_target_pairs={{0,16},{8,24},{16,0},{24,8},{1,17},{9,25},{17,1},{25,9},{2,18},{10... | collective-permute-start | bytes 1216520 | tf_op jit(solution)/shard_map/ppermute | solution.py:650
  158.8 35.0 %collective-permute-start.18 = (s16[528,384]{1,0:T(8,128)(2,1)}, s16[528,384]{1,0:T(8,128)(2,1)}, u32[]{:S(2)}, u32[]{:S(2)}) collective-permute-start(s16[528,384]{1,0:T(8,128)(2,1)} %get-tuple-element.65), channel_id=1, source_target_pairs={{0,16},{8,24},{16,0},{24,8},{1,17},{9,25},{17,1},{25,9},{2,18},{10... | collective-permute-start | bytes 1216520 | tf_op jit(solution)/shard_map/ppermute | solution.py:650
  162.1 48.2 %collective-permute-start.30 = (s16[528,384]{1,0:T(8,128)(2,1)S(1)}, s16[528,384]{1,0:T(8,128)(2,1)S(1)}, u32[]{:S(2)}, u32[]{:S(2)}) collective-permute-start(s16[528,384]{1,0:T(8,128)(2,1)S(1)} %get-tuple-element.83), channel_id=1, source_target_pairs={{0,16},{8,24},{16,0},{24,8},{1,17},{9,25},{17,1},{25,9},{2,18},{10... | collective-permute-start | bytes 1216520 | tf_op jit(solution)/shard_map/ppermute | solution.py:650
  227.2 43.0 %collective-permute-start.47 = (s16[528,384]{1,0:T(8,128)(2,1)}, s16[528,384]{1,0:T(8,128)(2,1)}, u32[]{:S(2)}, u32[]{:S(2)}) collective-permute-start(s16[528,384]{1,0:T(8,128)(2,1)} %copy-done.20), channel_id=1, source_target_pairs={{0,0},{1,8},{2,2},{3,10},{4,4},{5,12},{6,6},{7,14},{8,1},{9,9},{10... | collective-permute-start | bytes 1216520 | tf_op jit(solution)/shard_map/ppermute | solution.py:685
  246.3 20.7 %collective-permute-start.34 = (s16[400,512]{1,0:T(8,128)(2,1)S(1)}, s16[400,512]{1,0:T(8,128)(2,1)S(1)}, u32[]{:S(2)}, u32[]{:S(2)}) collective-permute-start(s16[400,512]{1,0:T(8,128)(2,1)S(1)} %get-tuple-element.95), channel_id=1, source_target_pairs={{0,17},{1,16},{2,19},{3,18},{4,21},{5,20},{6,23},{7,22},{8,25},{9,... | collective-permute-start | bytes 1228808 | tf_op jit(solution)/shard_map/ppermute | solution.py:727
  268.8 43.9 %collective-permute-start.43 = (s16[528,384]{1,0:T(8,128)(2,1)S(1)}, s16[528,384]{1,0:T(8,128)(2,1)S(1)}, u32[]{:S(2)}, u32[]{:S(2)}) collective-permute-start(s16[528,384]{1,0:T(8,128)(2,1)S(1)} %copy-done.19), channel_id=1, source_target_pairs={{0,0},{1,8},{2,2},{3,10},{4,4},{5,12},{6,6},{7,14},{8,1},{9,9},{10... | collective-permute-start | bytes 1216520 | tf_op jit(solution)/shard_map/ppermute | solution.py:685
  269.5 43.3 %collective-permute-start.45 = (s16[528,384]{1,0:T(8,128)(2,1)S(1)}, s16[528,384]{1,0:T(8,128)(2,1)S(1)}, u32[]{:S(2)}, u32[]{:S(2)}) collective-permute-start(s16[528,384]{1,0:T(8,128)(2,1)S(1)} %get-tuple-element.101), channel_id=1, source_target_pairs={{0,0},{1,8},{2,2},{3,10},{4,4},{5,12},{6,6},{7,14},{8,1},{9,9},{10... | collective-permute-start | bytes 1216520 | tf_op jit(solution)/shard_map/ppermute | solution.py:685
  270.2 43.3 %collective-permute-start.48 = (s16[528,384]{1,0:T(8,128)(2,1)}, s16[528,384]{1,0:T(8,128)(2,1)S(1)}, u32[]{:S(2)}, u32[]{:S(2)}) collective-permute-start(s16[528,384]{1,0:T(8,128)(2,1)} %collective-permute-done.47), channel_id=1, source_target_pairs={{0,0},{8,4},{2,8},{10,12},{4,16},{12,20},{6,24},{14,28},{1,1},{9,5... | collective-permute-start | bytes 1216520 | tf_op jit(solution)/shard_map/ppermute | solution.py:686
  308.3 37.8 %collective-permute-start.41 = (s16[4,112,512]{2,1,0:T(8,128)(2,1)S(1)}, s16[4,112,512]{2,1,0:T(8,128)(2,1)S(1)}, u32[]{:S(2)}, u32[]{:S(2)}) collective-permute-start(s16[4,112,512]{2,1,0:T(8,128)(2,1)S(1)} %shard_map.173.refs_0_), channel_id=1, source_target_pairs={{0,16},{1,17},{2,18},{3,19},{4,20},{5,21},{6,22},{7,23},{8,24},{9,... | collective-permute-start | bytes 1376264 | tf_op jit(solution)/shard_map/ppermute | solution.py:727
  308.4 37.7 %collective-permute-start.42 = (s16[4,112,512]{2,1,0:T(8,128)(2,1)S(1)}, s16[4,112,512]{2,1,0:T(8,128)(2,1)S(1)}, u32[]{:S(2)}, u32[]{:S(2)}) collective-permute-start(s16[4,112,512]{2,1,0:T(8,128)(2,1)S(1)} %shard_map.173.refs_0_), channel_id=1, source_target_pairs={{0,17},{1,16},{2,19},{3,18},{4,21},{5,20},{6,23},{7,22},{8,25},{9,... | collective-permute-start | bytes 1376264 | tf_op jit(solution)/shard_map/ppermute | solution.py:727
  312.7 33.4 %collective-permute-start.49 = (s16[4,112,512]{2,1,0:T(8,128)(2,1)S(1)}, s16[4,112,512]{2,1,0:T(8,128)(2,1)S(1)}, u32[]{:S(2)}, u32[]{:S(2)}) collective-permute-start(s16[4,112,512]{2,1,0:T(8,128)(2,1)S(1)} %shard_map.173.refs_0_), channel_id=1, source_target_pairs={{0,1},{1,0},{2,3},{3,2},{4,5},{5,4},{6,7},{7,6},{8,9},{9,8},{10,11... | collective-permute-start | bytes 1376264 | tf_op jit(solution)/shard_map/ppermute | solution.py:727
  319.5 27.5 %collective-permute-start.50 = (s16[4,112,512]{2,1,0:T(8,128)(2,1)S(1)}, s16[4,112,512]{2,1,0:T(8,128)(2,1)S(1)}, u32[]{:S(2)}, u32[]{:S(2)}) collective-permute-start(s16[4,112,512]{2,1,0:T(8,128)(2,1)S(1)} %shard_map.173.refs_0_), channel_id=1, source_target_pairs={{0,8},{8,0},{16,24},{24,16},{1,9},{9,1},{17,25},{25,17},{2,10},{10... | collective-permute-start | bytes 1376264 | tf_op jit(solution)/shard_map/ppermute | solution.py:744
  (70 other events, 812.4 us)
